TPU v7x, 32 devices: a whole 2x2x4 slice. The times are simulated.
32 devices in a mesh: gx: 8 (over y, x, core), gy: 4 (over z).
Axes of the slice: x: 2, y: 2, z: 4, core: 2. Of those that a mesh axis runs over, the one named last changes fastest.
Arguments:
- x_first: bfloat16 [128, 16384], P(None, 'gx'), may hold values from -160 to 160
- x_second: bfloat16 [128, 16384], P(None, 'gx'), may hold values from -160 to 160
- norm_gain: bfloat16 [16384], P('gx'), may hold values from 0.25 to 1.75
- w_qkv: bfloat16 [16384, 18432], P('gx', 'gy'), may hold values from -0.046875 to 0.046875
- w_out: bfloat16 [16384, 16384], P('gy', 'gx'), may hold values from -0.046875 to 0.046875
- cache_keys: bfloat16 [128, 768, 1024], P(('gx', 'gy')), may hold values from -240 to 240
- cache_values: bfloat16 [128, 768, 1024], P(('gx', 'gy')), may hold values from -8 to 8
- lengths: int32 [128], P(('gx', 'gy')), may hold values from 1 to 768, as said below
Outputs:
- out_first: bfloat16 [128, 16384], P('gy', 'gx')
- out_second: bfloat16 [128, 16384], P('gy', 'gx')
Inputs may be any that keep to these rules, and one draw needn't show every extreme that they name: `lengths`: some sequence has exactly 768 filled slots in every draw.
All inputs are finite; a program needn't handle non-finite values.
Results may differ from a plain program's by a relative error of at most 0.012.
The roundings to bfloat16 on the way count: a program that leaves them out, or rounds other values in their place, can miss the bound.
Values may be sent and summed in bfloat16 or wider, within the bound.
A program may use at most 192 MiB of HBM per device.

v0:
```python
import functools
import math

import jax
import jax.numpy as jnp
from jax import lax
from jax.experimental import pallas as pl
from jax.experimental.pallas import tpu as pltpu
from jax.sharding import PartitionSpec as P

HD = 128
norm_eps = 1e-05
rotary_base = 500000.0
STEPS = 2
VMEM_LIMIT = 60 * 1024 * 1024


def qkv_kernel(heads_per, x_ref, gain_ref, w_ref, out_ref, scaled_ref):
    step = pl.program_id(0)
    last = pl.num_programs(0) - 1
    outer, inner, _, tile, _ = out_ref.shape

    @pl.when(step == 0)
    def _():
        scaled_ref[...] = (
            x_ref[...].astype(jnp.float32) * gain_ref[...].astype(jnp.float32)
        ).astype(jnp.bfloat16)

    @pl.when(step < last)
    def _():
        product = jnp.dot(scaled_ref[...], w_ref[...], preferred_element_type=jnp.float32)
        for h in range(heads_per):
            out_ref[:, :, h] = product[:, h * HD : (h + 1) * HD].reshape(outer, inner, tile, HD)

    @pl.when(step == last)
    def _():
        wide = x_ref[...].astype(jnp.float32)
        squares = jnp.sum(wide * wide, axis=1, keepdims=True)
        lanes = jnp.broadcast_to(squares, (squares.shape[0], HD)).reshape(outer, inner, tile, HD)
        for h in range(heads_per):
            out_ref[:, :, h] = lanes


def qkv_partial(x, gain, w, outer, inner):
    rows, depth = x.shape
    columns = w.shape[1]
    heads_per = 2
    width = heads_per * HD
    blocks = columns // width
    tile = rows // (outer * inner)
    return pl.pallas_call(
        functools.partial(qkv_kernel, heads_per),
        grid=(blocks + 1,),
        in_specs=[
            pl.BlockSpec((rows, depth), lambda n: (0, 0)),
            pl.BlockSpec((1, depth), lambda n: (0, 0)),
            pl.BlockSpec((depth, width), lambda n: (0, jnp.minimum(n, blocks - 1))),
        ],
        out_specs=pl.BlockSpec(
            (outer, inner, heads_per, tile, HD), lambda n: (0, 0, n, 0, 0)
        ),
        out_shape=jax.ShapeDtypeStruct(
            (outer, inner, columns // HD + heads_per, tile, HD), jnp.float32
        ),
        scratch_shapes=[pltpu.VMEM((rows, depth), jnp.bfloat16)],
        compiler_params=pltpu.CompilerParams(vmem_limit_bytes=VMEM_LIMIT),
    )(x, gain, w)


def attend_kernel(
    groups, size, rows, lengths_ref, x_ref, cos_ref, sin_ref, keys_ref, values_ref, out_ref,
    in_ref, mix_ref,
):
    row = pl.program_id(0)
    tile = STEPS * rows
    per = size + 2
    slots = keys_ref.shape[1]
    scale = 1.0 / math.sqrt(HD)

    @pl.when(row == 0)
    def _():
        for k in range(groups):
            base = k * per
            turn = x_ref[base : base + size + 1].astype(jnp.float32)
            turned = turn * cos_ref[...][None] + pltpu.roll(turn, HD // 2, 2) * sin_ref[...][None]
            turned = turned.astype(jnp.bfloat16).astype(jnp.float32)
            in_ref[base * tile : (base + size + 1) * tile] = turned.reshape((size + 1) * tile, HD)
            in_ref[(base + size + 1) * tile : (base + per) * tile] = x_ref[base + size + 1].astype(
                jnp.float32
            )

    length = lengths_ref[row]
    valid = lax.broadcasted_iota(jnp.int32, (1, slots), 1) < length
    late = lax.broadcasted_iota(jnp.int32, (STEPS * size, 1), 0) >= size
    for k in range(groups):
        base = k * per * tile
        query = jnp.concatenate(
            [
                in_ref[pl.ds(base + s * rows + row, size, stride=tile), :]
                for s in range(STEPS)
            ],
            axis=0,
        )
        new_keys = [in_ref[pl.ds(base + size * tile + s * rows + row, 1), :] for s in range(STEPS)]
        new_values = [
            in_ref[pl.ds(base + (size + 1) * tile + s * rows + row, 1), :] for s in range(STEPS)
        ]
        columns = slice(k * HD, (k + 1) * HD)
        scores = (
            lax.dot_general(
                query.astype(jnp.bfloat16),
                keys_ref[0, :, columns],
                (((1,), (1,)), ((), ())),
                preferred_element_type=jnp.float32,
            )
            * scale
        )
        scores = jnp.where(valid, scores, -jnp.inf)
        extra_one = jnp.sum(query * new_keys[0], axis=1, keepdims=True) * scale
        extra_two = jnp.sum(query * new_keys[1], axis=1, keepdims=True) * scale
        extra_two = jnp.where(late, extra_two, -jnp.inf)
        top = jnp.maximum(
            jnp.max(scores, axis=1, keepdims=True), jnp.maximum(extra_one, extra_two)
        )
        weights = jnp.exp(scores - top)
        weight_one = jnp.exp(extra_one - top)
        weight_two = jnp.exp(extra_two - top)
        total = jnp.sum(weights, axis=1, keepdims=True) + weight_one + weight_two
        mixed = jnp.dot(
            weights.astype(jnp.bfloat16),
            values_ref[0, :, columns],
            preferred_element_type=jnp.float32,
        )
        mixed = (
            mixed
            + weight_one.astype(jnp.bfloat16).astype(jnp.float32) * new_values[0]
            + weight_two.astype(jnp.bfloat16).astype(jnp.float32) * new_values[1]
        )
        mixed = mixed / total
        for s in range(STEPS):
            mix_ref[pl.ds(k * size * tile + s * rows + row, size, stride=tile), :] = mixed[
                s * size : (s + 1) * size
            ]

    @pl.when(row == rows - 1)
    def _():
        out_ref[...] = mix_ref[...].reshape(out_ref.shape).astype(jnp.bfloat16)


def attend(joined, cosine, sine, keys, values, lengths):
    rows, slots, width = keys.shape
    groups = width // HD
    heads, tile, _ = joined.shape
    size = heads // groups - 2
    whole = lambda r, lens: (0, 0)
    return pl.pallas_call(
        functools.partial(attend_kernel, groups, size, rows),
        grid_spec=pltpu.PrefetchScalarGridSpec(
            num_scalar_prefetch=1,
            grid=(rows,),
            in_specs=[
                pl.BlockSpec((heads, tile, HD), lambda r, lens: (0, 0, 0)),
                pl.BlockSpec((tile, HD), whole),
                pl.BlockSpec((tile, HD), whole),
                pl.BlockSpec((1, slots, width), lambda r, lens: (r, 0, 0)),
                pl.BlockSpec((1, slots, width), lambda r, lens: (r, 0, 0)),
            ],
            out_specs=pl.BlockSpec((groups * size, tile, HD), lambda r, lens: (0, 0, 0)),
            scratch_shapes=[
                pltpu.VMEM((heads * tile, HD), jnp.float32),
                pltpu.VMEM((groups * size * tile, HD), jnp.float32),
            ],
        ),
        out_shape=jax.ShapeDtypeStruct((groups * size, tile, HD), jnp.bfloat16),
        compiler_params=pltpu.CompilerParams(vmem_limit_bytes=VMEM_LIMIT),
    )(lengths, joined, cosine, sine, keys, values)


def out_kernel(x_ref, w_ref, out_ref, flat_ref):
    @pl.when(pl.program_id(0) == 0)
    def _():
        for h in range(x_ref.shape[2]):
            flat_ref[:, h * HD : (h + 1) * HD] = (
                x_ref[:, :, h].astype(jnp.float32).reshape(flat_ref.shape[0], HD)
            ).astype(jnp.bfloat16)

    out_ref[...] = jnp.dot(flat_ref[...], w_ref[...], preferred_element_type=jnp.float32)


def out_partial(heads, w):
    outer, inner, count, tile, _ = heads.shape
    rows = outer * inner * tile
    depth, columns = w.shape
    width = min(256, columns)
    return pl.pallas_call(
        out_kernel,
        grid=(columns // width,),
        in_specs=[
            pl.BlockSpec(heads.shape, lambda n: (0, 0, 0, 0, 0)),
            pl.BlockSpec((depth, width), lambda n: (0, n)),
        ],
        out_specs=pl.BlockSpec((rows, width), lambda n: (0, n)),
        out_shape=jax.ShapeDtypeStruct((rows, columns), jnp.float32),
        scratch_shapes=[pltpu.VMEM((rows, depth), jnp.bfloat16)],
        compiler_params=pltpu.CompilerParams(vmem_limit_bytes=VMEM_LIMIT),
    )(heads, w)


def body(x_first, x_second, norm_gain, w_qkv, w_out, cache_keys, cache_values, lengths):
    outer, inner = lax.axis_size("gx"), lax.axis_size("gy")
    rows = lengths.shape[0]
    tile = STEPS * rows
    depth = x_first.shape[1]
    width = depth * outer
    heads_here = w_qkv.shape[1] // HD

    stacked = jnp.stack(
        [x.reshape(outer * inner, rows, depth) for x in (x_first, x_second)], axis=1
    ).reshape(outer * inner * tile, depth)
    half = HD // 2
    freq = rotary_base ** (-(jnp.arange(half, dtype=jnp.float32) * 2.0 / HD))
    position = jnp.concatenate([lengths + s for s in range(STEPS)])
    angle = position.astype(jnp.float32)[:, None] * freq
    cosine = jnp.tile(jnp.cos(angle), (1, 2))
    sine = jnp.concatenate([-jnp.sin(angle), jnp.sin(angle)], axis=1)

    partial_sum = qkv_partial(stacked, norm_gain[None], w_qkv, outer, inner)
    summed = lax.psum_scatter(partial_sum, "gx", scatter_dimension=0, tiled=True)[0]
    squares = summed[:, heads_here : heads_here + 1]
    joined = (summed[:, :heads_here] * lax.rsqrt(squares / width + norm_eps)).astype(jnp.bfloat16)
    joined = lax.all_to_all(joined, "gy", split_axis=0, concat_axis=0, tiled=True)
    joined = joined.reshape(inner * heads_here, tile, HD)

    heads = attend(joined, cosine, sine, cache_keys, cache_values, lengths)
    heads = heads.reshape(inner, heads.shape[0] // inner, tile, HD)
    heads = lax.all_to_all(heads, "gy", split_axis=0, concat_axis=0, tiled=True)
    heads = lax.all_gather(heads, "gx", axis=0, tiled=False)
    partial_out = out_partial(heads, w_out)
    done = lax.psum_scatter(partial_out, "gy", scatter_dimension=0, tiled=True)
    done = done.astype(jnp.bfloat16).reshape(-1, STEPS, rows, partial_out.shape[1])
    return tuple(done[:, s].reshape(-1, partial_out.shape[1]) for s in range(STEPS))


def solution(mesh):
    in_specs = (
        P(None, "gx"),
        P(None, "gx"),
        P("gx"),
        P("gx", "gy"),
        P("gy", "gx"),
        P(("gx", "gy"), None, None),
        P(("gx", "gy"), None, None),
        P(("gx", "gy")),
    )
    out_specs = (P("gy", "gx"), P("gy", "gx"))
    return jax.shard_map(body, mesh=mesh, in_specs=in_specs, out_specs=out_specs, check_vma=False)
```

profile of v0, /device:TPU:0, one launch (start us, length us, event | category | flops | bytes accessed | tf_op | source)
XLA Modules:
  0.0 223.7 jit_solution(13736544586612227737)
XLA Ops:
  7.2 0.0 copy-start.1
  7.2 0.0 reduce-scatter.3.cloned.1.call-start
  7.2 1.2 stack_reshape.7
  8.5 1.2 stack_reshape.6
  9.7 0.7 pad_maximum_fusion
  10.4 1.1 reshape.67.x_ref
  11.5 0.6 broadcast_in_dim.2.gain_ref
  12.1 18.7 %shard_map.95 = f32[8,4,38,8,128]{4,3,2,1,0:T(8,128)} custom-call(bf16[256,2048]{1,0:T(8,128)(2,1)} %reshape.67.x_ref, bf16[1,2048]{1,0:T(2,128)(2,1)} %broadcast_in_dim.2.gain_ref, bf16[2048,4608]{1,0:T(8,128)(2,1)} %w_ref.2), custom_call_target="tpu_custom_call" | custom-call | tf_op jit(solution)/shard_map/pallas_call | solution.py:51
  30.9 0.0 reduce-scatter.3.cloned.1.call-update
  30.9 57.9 %reduce-scatter.3.cloned.1.call-done = f32[1,4,38,8,128]{4,3,2,1,0:T(8,128)} async-done(((f32[8,4,38,8,128]{4,3,2,1,0:T(8,128)}), f32[1,4,38,8,128]{4,3,2,1,0:T(8,128)}) %reduce-scatter.3.cloned.1.call-update) | async-done | bytes 622608 | tf_op jit(solution)/shard_map/reduce_scatter | solution.py:228
  88.9 0.7 fusion.3
  89.6 1.8 fusion
  91.4 4.6 %all-to-all-start = ((bf16[4,36,8,128]{3,2,1,0:T(8,128)(2,1)}), bf16[4,36,8,128]{3,2,1,0:T(8,128)(2,1)S(1)}, u32[]{:S(2)}, u32[]{:S(2)}) async-start(bf16[4,36,8,128]{3,2,1,0:T(8,128)(2,1)} %fusion), calls=%async_computation.1 | async-start | bytes 589824 | tf_op jit(solution)/shard_map/all_to_all | solution.py:231
  96.1 0.1 add_convert_fusion
  96.1 0.1 fusion.4
  96.3 0.7 tile.10.cos_ref
  96.9 0.7 pad_maximum_fusion.1.sin_ref
  97.6 8.1 %all-to-all-done = bf16[4,36,8,128]{3,2,1,0:T(8,128)(2,1)S(1)} async-done(((bf16[4,36,8,128]{3,2,1,0:T(8,128)(2,1)}), bf16[4,36,8,128]{3,2,1,0:T(8,128)(2,1)S(1)}, u32[]{:S(2)}, u32[]{:S(2)}) %all-to-all-start) | async-done | bytes 294944 | tf_op jit(solution)/shard_map/all_to_all | solution.py:231
  105.7 0.7 copy-done
  106.4 13.8 %shard_map.96 = bf16[128,8,128]{2,1,0:T(8,128)(2,1)} custom-call(s32[4]{0:T(128)} %lengths_ref.1, bf16[144,8,128]{2,1,0:T(8,128)(2,1)} %bitcast.11, f32[8,128]{1,0:T(8,128)} %tile.10.cos_ref, f32[8,128]{1,0:T(8,128)} %pad_maximum_fusion.1.sin_ref, bf16[4,768,1024]{2,1,0:T(8,128)(2,1)} %keys_ref.1, bf16[4,768,1024]{2,1,0:T(8,128)(2,1)} %values_ref.1), custom_call_target="tpu_custom_call" | custom-call | tf_op jit(solution)/shard_map/pallas_call | solution.py:156
  120.2 11.3 %all_to_all.10 = bf16[4,32,8,128]{3,2,1,0:T(8,128)(2,1)} all-to-all(bf16[4,32,8,128]{3,2,1,0:T(8,128)(2,1)} %bitcast.12), channel_id=1, replica_groups=mesh['gx'=8,'gy'=4] {'gy'}, dimensions={0} | all-to-all | bytes 524288 | tf_op jit(solution)/shard_map/all_to_all | solution.py:236
  131.5 0.0 all-gather.3.cloned.1.call-update
  131.5 0.0 reduce-scatter.5.cloned.1.call-start
  131.5 26.3 %all-gather.3.cloned.1.call-done = bf16[32,32,8,128]{3,2,1,0:T(8,128)(2,1)} async-done(((bf16[4,32,8,128]{3,2,1,0:T(8,128)(2,1)}), bf16[32,32,8,128]{3,2,1,0:T(8,128)(2,1)}) %all-gather.3.cloned.1.call-update) | async-done | bytes 2097168 | tf_op jit(solution)/shard_map/all_gather | solution.py:237
  157.8 12.7 %shard_map.97 = f32[256,2048]{1,0:T(8,128)} custom-call(bf16[8,4,32,8,128]{4,3,2,1,0:T(8,128)(2,1)} %bitcast.8, bf16[4096,2048]{1,0:T(8,128)(2,1)} %w_ref.3), custom_call_target="tpu_custom_call" | custom-call | tf_op jit(solution)/shard_map/pallas_call | solution.py:195
  170.5 0.0 reduce-scatter.5.cloned.1.call-update
  170.5 44.0 %reduce-scatter.5.cloned.1.call-done = f32[64,2048]{1,0:T(8,128)} async-done(((f32[256,2048]{1,0:T(8,128)}), f32[64,2048]{1,0:T(8,128)}) %reduce-scatter.5.cloned.1.call-update) | async-done | bytes 524304 | tf_op jit(solution)/shard_map/reduce_scatter | solution.py:239
  214.5 1.1 convert_element_type.15
  215.6 0.1 reshape.70
  215.7 0.1 fusion.5
  215.8 0.7 reshape_squeeze.6
  216.5 0.7 reshape_squeeze.7
  (8 shorter events, 0.0 us)
Async XLA Ops:
  7.2 4.4 %copy-start.1 = (bf16[2048]{0:T(1024)(128)(2,1)S(1)}, bf16[2048]{0:T(1024)(128)(2,1)}, u32[]{:S(2)}) copy-start(bf16[2048]{0:T(1024)(128)(2,1)} %param.10) | copy-start | bytes 12292
  7.2 81.7 %reduce-scatter.3.cloned.1.call-start = ((), (), s32[]{:S(2)}) async-start(), calls=%async_computation.4 | async-start | bytes 5603328 | tf_op jit(solution)/shard_map/reduce_scatter | solution.py:228
  12.1 18.8 %copy-start.2 = (s32[4]{0:T(128)S(1)}, s32[4]{0:T(128)}, u32[]{:S(2)}) copy-start(s32[4]{0:T(128)} %lengths_ref.1) | copy-start | bytes 52
  91.4 14.2 %all-to-all-start = ((bf16[4,36,8,128]{3,2,1,0:T(8,128)(2,1)}), bf16[4,36,8,128]{3,2,1,0:T(8,128)(2,1)S(1)}, u32[]{:S(2)}, u32[]{:S(2)}) async-start(bf16[4,36,8,128]{3,2,1,0:T(8,128)(2,1)} %fusion), calls=%async_computation.1 | async-start | bytes 589824 | tf_op jit(solution)/shard_map/all_to_all | solution.py:231
  96.0 61.8 %all-gather.3.cloned.1.call-start = ((), (), s32[]{:S(2)}) async-start(), calls=%async_computation.6 | async-start | bytes 2359296 | tf_op jit(solution)/shard_map/all_gather | solution.py:237
  105.7 0.7 copy-start
  131.5 83.0 %reduce-scatter.5.cloned.1.call-start = ((), (), s32[]{:S(2)}) async-start(), calls=%async_computation.5 | async-start | bytes 2621440 | tf_op jit(solution)/shard_map/reduce_scatter | solution.py:239
Sparse Core Ops, SparseCore 0:
  31.0 57.8 reduce-scatter.2
  131.6 26.1 all-gather.2
  170.6 43.8 reduce-scatter.4
where the time goes:
time: 225 us; the launch traced here: 224 us
  waiting for transfers between devices  136 us (60%)
  Pallas kernels  45.2 us (20%)
  between operations  13.8 us (6%)
  blocking collectives  11.3 us (5%)
  local copies, waits for them, and re-layouts  7.2 us (3%)
  other arithmetic  5.18 us (2%)
  starting transfers between devices  4.69 us (2%)
    reduce_scatter x1, waiting for transfers between devices, body(): lax.psum_scatter(partial_sum, 'gx', scatter_dimension=0, tiled=True)[0]  57.9 us
    reduce_scatter x1, waiting for transfers between devices, body(): done = lax.psum_scatter(partial_out, 'gy', scatter_dimension=0, tiled=True)  44 us
    all_gather x1, waiting for transfers between devices, body(): heads = lax.all_gather(heads, 'gx', axis=0, tiled=False)  26.3 us
    pallas_call x1, Pallas kernels, qkv_partial(): pl.pallas_call(functools.partial(qkv_kernel, heads_per), grid=(blocks + 1...  18.7 us
    pallas_call x1, Pallas kernels, attend(): pl.pallas_call(functools.partial(attend_kernel, groups, size, rows), grid...  13.8 us
    pallas_call x1, Pallas kernels, out_partial(): pl.pallas_call(out_kernel, grid=(columns // width,), in_specs=[pl.BlockSp...  12.7 us
    all_to_all x1, blocking collectives, body(): heads = lax.all_to_all(heads, 'gy', split_axis=0, concat_axis=0, tiled=True)  11.3 us
    all_to_all x1, waiting for transfers between devices, body(): lax.all_to_all(joined, 'gy', split_axis=0, concat_axis=0, tiled=True)  8.08 us
  transfers between devices with their start and end apart: 4, of which 4 were waited for; matrix products, arithmetic and copies ran while one was open for 1% of the time, Pallas kernels for 0%

commit v1 on v0

--- a/solution.py
+++ b/solution.py
@@ -15,56 +15,208 @@
 VMEM_LIMIT = 60 * 1024 * 1024
 
 
-def qkv_kernel(heads_per, x_ref, gain_ref, w_ref, out_ref, scaled_ref):
-    step = pl.program_id(0)
-    last = pl.num_programs(0) - 1
-    outer, inner, _, tile, _ = out_ref.shape
-
-    @pl.when(step == 0)
-    def _():
-        scaled_ref[...] = (
-            x_ref[...].astype(jnp.float32) * gain_ref[...].astype(jnp.float32)
-        ).astype(jnp.bfloat16)
-
-    @pl.when(step < last)
-    def _():
-        product = jnp.dot(scaled_ref[...], w_ref[...], preferred_element_type=jnp.float32)
-        for h in range(heads_per):
-            out_ref[:, :, h] = product[:, h * HD : (h + 1) * HD].reshape(outer, inner, tile, HD)
-
-    @pl.when(step == last)
-    def _():
-        wide = x_ref[...].astype(jnp.float32)
-        squares = jnp.sum(wide * wide, axis=1, keepdims=True)
-        lanes = jnp.broadcast_to(squares, (squares.shape[0], HD)).reshape(outer, inner, tile, HD)
-        for h in range(heads_per):
-            out_ref[:, :, h] = lanes
-
-
-def qkv_partial(x, gain, w, outer, inner):
-    rows, depth = x.shape
-    columns = w.shape[1]
-    heads_per = 2
-    width = heads_per * HD
-    blocks = columns // width
-    tile = rows // (outer * inner)
+MESH = pl.DeviceIdType.MESH
+
+
+def signal_peers(peers):
+    barrier = pltpu.get_barrier_semaphore()
+    for peer in peers:
+        pl.semaphore_signal(barrier, inc=1, device_id=peer, device_id_type=MESH)
+    pl.semaphore_wait(barrier, len(peers))
+
+
+def places(outer, inner):
+    gx, gy = lax.axis_index("gx"), lax.axis_index("gy")
+    pairs = outer // 2
+    pair, side = gx // 2, lax.rem(gx, 2)
+    other = (gx + 1 - 2 * side, gy)
+    along = [(2 * lax.rem(pair + d, pairs) + side, gy) for d in range(1, pairs)]
+    across = [(gx, lax.rem(gy + d, inner)) for d in range(1, inner)]
+    return gx, gy, pair, side, other, along, across
+
+
+def project_kernel(
+    dims, x_first, x_second, gain, w, out,
+    scaled, w_here, prod, from_other, to_along, from_along, sq, sq_other, sq_to, sq_along,
+    mixed, to_across, w_sem, pair_send, pair_recv, along_send, along_recv, across_send,
+    across_recv, sq_send, sq_recv, sqa_send, sqa_recv, own_sem,
+):
+    outer, inner, rows, width, chunk_heads, chunks = dims
+    gx, gy, pair, side, other, along, across = places(outer, inner)
+    pairs = outer // 2
+    cw = chunk_heads * HD
+    block = inner * rows
+    tile = STEPS * rows
+
+    def w_copy(n):
+        return pltpu.make_async_copy(w.at[:, pl.ds(n * cw, cw)], w_here.at[n], w_sem.at[n])
+
+    for n in range(chunks):
+        w_copy(n).start()
+    signal_peers([other] + along + across)
+
+    wide_gain = gain[...].astype(jnp.float32)
+    for s, x in enumerate((x_first, x_second)):
+
+        @pl.loop(0, outer)
+        def _(g):
+            wide = x[pl.ds(g * block, block), :].astype(jnp.float32)
+            row = g * STEPS * block + s * block
+            scaled[pl.ds(row, block), :] = (wide * wide_gain).astype(jnp.bfloat16)
+            total = jnp.sum(wide * wide, axis=1, keepdims=True)
+            sq[g // 2, g % 2, s * block : (s + 1) * block, :] = jnp.broadcast_to(
+                total, (block, HD)
+            )
+
+    def send_sq():
+        return pltpu.make_async_remote_copy(
+            src_ref=sq.at[:, 1 - side], dst_ref=sq_other, send_sem=sq_send, recv_sem=sq_recv,
+            device_id=other, device_id_type=MESH,
+        )
+
+    def send_pair(n):
+        return pltpu.make_async_remote_copy(
+            src_ref=prod.at[n, :, 1 - side], dst_ref=from_other.at[n],
+            send_sem=pair_send.at[n], recv_sem=pair_recv.at[n],
+            device_id=other, device_id_type=MESH,
+        )
+
+    def send_along(n, d):
+        return pltpu.make_async_remote_copy(
+            src_ref=to_along.at[n, d], dst_ref=from_along.at[n, d],
+            send_sem=along_send.at[n, d], recv_sem=along_recv.at[n, d],
+            device_id=along[d], device_id_type=MESH,
+        )
+
+    def send_sq_along(d):
+        return pltpu.make_async_remote_copy(
+            src_ref=sq_to.at[d], dst_ref=sq_along.at[d],
+            send_sem=sqa_send.at[d], recv_sem=sqa_recv.at[d],
+            device_id=along[d], device_id_type=MESH,
+        )
+
+    def send_across(n, d):
+        return pltpu.make_async_remote_copy(
+            src_ref=to_across.at[n, lax.rem(gy + d + 1, inner)],
+            dst_ref=out.at[gy, pl.ds(n * chunk_heads, chunk_heads)],
+            send_sem=across_send.at[n, d], recv_sem=across_recv.at[n, d],
+            device_id=across[d], device_id_type=MESH,
+        )
+
+    def keep_own(n):
+        return pltpu.make_async_copy(
+            to_across.at[n, gy], out.at[gy, pl.ds(n * chunk_heads, chunk_heads)], own_sem.at[n]
+        )
+
+    send_sq().start()
+
+    def pass_on(n):
+        send_pair(n).wait()
+        for d in range(pairs - 1):
+            there = lax.rem(pair + d + 1, pairs)
+            to_along[n, d] = (prod[n, there, side] + from_other[n, there]).astype(jnp.bfloat16)
+            send_along(n, d).start()
+
+    @pl.loop(0, chunks)
+    def _(n):
+        w_copy(n).wait()
+        product = jnp.dot(scaled[...], w_here[n], preferred_element_type=jnp.float32)
+        prod[n] = product.reshape(pairs, 2, STEPS * block, cw)
+        send_pair(n).start()
+
+        @pl.when(n == 0)
+        def _():
+            send_sq().wait()
+            for d in range(pairs - 1):
+                there = lax.rem(pair + d + 1, pairs)
+                sq_to[d] = sq[there, side] + sq_other[there]
+                send_sq_along(d).start()
+
+        @pl.when(n > 0)
+        def _():
+            pass_on(n - 1)
+
+    pass_on(chunks - 1)
+
+    squares = sq[pair, side] + sq_other[pair]
+    for d in range(pairs - 1):
+        send_sq_along(d).wait()
+        squares = squares + sq_along[d]
+    factor = lax.rsqrt(squares / width + norm_eps)
+    sq[0, 0] = factor
+
+    @pl.loop(0, chunks)
+    def _(n):
+        for d in range(pairs - 1):
+            send_along(n, d).wait()
+        for h in range(chunk_heads):
+            columns = slice(h * HD, (h + 1) * HD)
+            total = prod[n, pair, side, :, columns] + from_other[n, pair, :, columns]
+            for d in range(pairs - 1):
+                total = total + from_along[n, d, :, columns].astype(jnp.float32)
+            total = total * sq[0, 0]
+            for s in range(STEPS):
+                for z in range(inner):
+                    mixed[h, z * tile + s * rows : z * tile + (s + 1) * rows, :] = total[
+                        s * block + z * rows : s * block + (z + 1) * rows
+                    ]
+            for z in range(inner):
+                to_across[n, z, h] = mixed[h, z * tile : (z + 1) * tile, :].astype(jnp.bfloat16)
+        for d in range(inner - 1):
+            send_across(n, d).start()
+        keep_own(n).start()
+
+    @pl.loop(0, chunks)
+    def _(n):
+        keep_own(n).wait()
+        for d in range(inner - 1):
+            send_across(n, d).wait()
+
+
+def project(x_first, x_second, gain, w, outer, inner, rows, width):
+    depth, columns = w.shape
+    heads = columns // HD
+    chunk_heads = 6
+    chunks = heads // chunk_heads
+    cw = chunk_heads * HD
+    pairs = outer // 2
+    here = STEPS * inner * rows
+    tile = STEPS * rows
+    dims = (outer, inner, rows, width, chunk_heads, chunks)
+    dma = pltpu.SemaphoreType.DMA
+    vmem = pl.BlockSpec(memory_space=pltpu.VMEM)
+    f32, b16 = jnp.float32, jnp.bfloat16
     return pl.pallas_call(
-        functools.partial(qkv_kernel, heads_per),
-        grid=(blocks + 1,),
-        in_specs=[
-            pl.BlockSpec((rows, depth), lambda n: (0, 0)),
-            pl.BlockSpec((1, depth), lambda n: (0, 0)),
-            pl.BlockSpec((depth, width), lambda n: (0, jnp.minimum(n, blocks - 1))),
+        functools.partial(project_kernel, dims),
+        in_specs=[vmem, vmem, vmem, pl.BlockSpec(memory_space=pl.ANY)],
+        out_specs=vmem,
+        out_shape=jax.ShapeDtypeStruct((inner, heads, tile, HD), b16),
+        scratch_shapes=[
+            pltpu.VMEM((outer * here, depth), b16),
+            pltpu.VMEM((chunks, depth, cw), b16),
+            pltpu.VMEM((chunks, pairs, 2, here, cw), f32),
+            pltpu.VMEM((chunks, pairs, here, cw), f32),
+            pltpu.VMEM((chunks, pairs - 1, here, cw), b16),
+            pltpu.VMEM((chunks, pairs - 1, here, cw), b16),
+            pltpu.VMEM((pairs, 2, here, HD), f32),
+            pltpu.VMEM((pairs, here, HD), f32),
+            pltpu.VMEM((pairs - 1, here, HD), f32),
+            pltpu.VMEM((pairs - 1, here, HD), f32),
+            pltpu.VMEM((chunk_heads, here, HD), f32),
+            pltpu.VMEM((chunks, inner, chunk_heads, tile, HD), b16),
+            dma((chunks,)),
+            dma((chunks,)), dma((chunks,)),
+            dma((chunks, pairs - 1)), dma((chunks, pairs - 1)),
+            dma((chunks, inner - 1)), dma((chunks, inner - 1)),
+            dma, dma,
+            dma((pairs - 1,)), dma((pairs - 1,)),
+            dma((chunks,)),
         ],
-        out_specs=pl.BlockSpec(
-            (outer, inner, heads_per, tile, HD), lambda n: (0, 0, n, 0, 0)
+        compiler_params=pltpu.CompilerParams(
+            collective_id=0, has_side_effects=True, vmem_limit_bytes=VMEM_LIMIT
         ),
-        out_shape=jax.ShapeDtypeStruct(
-            (outer, inner, columns // HD + heads_per, tile, HD), jnp.float32
-        ),
-        scratch_shapes=[pltpu.VMEM((rows, depth), jnp.bfloat16)],
-        compiler_params=pltpu.CompilerParams(vmem_limit_bytes=VMEM_LIMIT),
-    )(x, gain, w)
+        name="project",
+    )(x_first, x_second, gain, w)
 
 
 def attend_kernel(
@@ -176,33 +328,162 @@
     )(lengths, joined, cosine, sine, keys, values)
 
 
-def out_kernel(x_ref, w_ref, out_ref, flat_ref):
-    @pl.when(pl.program_id(0) == 0)
-    def _():
-        for h in range(x_ref.shape[2]):
-            flat_ref[:, h * HD : (h + 1) * HD] = (
-                x_ref[:, :, h].astype(jnp.float32).reshape(flat_ref.shape[0], HD)
-            ).astype(jnp.bfloat16)
-
-    out_ref[...] = jnp.dot(flat_ref[...], w_ref[...], preferred_element_type=jnp.float32)
-
-
-def out_partial(heads, w):
-    outer, inner, count, tile, _ = heads.shape
-    rows = outer * inner * tile
+def finish_kernel(
+    dims, heads, w, out_first, out_second,
+    held, flat, w_here, own, to_across, from_across, piece,
+    w_sem, z_send, z_recv, keep_sem, along_send, along_recv, share_send, share_recv,
+    across_send, across_recv,
+):
+    outer, inner, rows, chunks = dims
+    gx, gy, pair, side, other, along, across = places(outer, inner)
+    pairs = outer // 2
+    count = heads.shape[1]
+    tile = STEPS * rows
+    cw = w_here.shape[2]
+    depth = flat.shape[1]
+    part = flat.shape[0] // inner
+    groups = part // tile
+
+    def w_copy(n):
+        return pltpu.make_async_copy(w.at[:, pl.ds(n * cw, cw)], w_here.at[n], w_sem.at[n])
+
+    for n in range(chunks):
+        w_copy(n).start()
+    signal_peers([other] + along + across)
+
+    def send_z(d):
+        return pltpu.make_async_remote_copy(
+            src_ref=heads.at[lax.rem(gy + d + 1, inner)], dst_ref=held.at[gx, gy],
+            send_sem=z_send.at[d], recv_sem=z_recv.at[d],
+            device_id=across[d], device_id_type=MESH,
+        )
+
+    def source(d):
+        return lax.rem(gy + inner - d, inner)
+
+    def send_along(d, e):
+        return pltpu.make_async_remote_copy(
+            src_ref=held.at[gx, source(d)], dst_ref=held.at[gx, source(d)],
+            send_sem=along_send.at[d, e], recv_sem=along_recv.at[d, e],
+            device_id=along[e], device_id_type=MESH,
+        )
+
+    def share(d, e):
+        column = 2 * lax.rem(pair + pairs - e, pairs) + side
+        return pltpu.make_async_remote_copy(
+            src_ref=held.at[column, source(d)], dst_ref=held.at[column, source(d)],
+            send_sem=share_send.at[d, e], recv_sem=share_recv.at[d, e],
+            device_id=other, device_id_type=MESH,
+        )
+
+    keep = pltpu.make_async_copy(heads.at[gy], held.at[gx, gy], keep_sem)
+    keep.start()
+    for d in range(inner - 1):
+        send_z(d).start()
+    keep.wait()
+    for d in range(inner):
+        if d > 0:
+            send_z(d - 1).wait_recv()
+        for e in range(pairs - 1):
+            send_along(d, e).start()
+        share(d, 0).start()
+    for d in range(inner):
+        for e in range(pairs - 1):
+            send_along(d, e).wait_recv()
+            share(d, e + 1).start()
+    for d in range(inner):
+        for e in range(pairs):
+            share(d, e).wait_recv()
+
+    @pl.loop(0, outer)
+    def _(g):
+        for h in range(count):
+            flat[pl.ds(g * inner * tile, inner * tile), h * HD : (h + 1) * HD] = (
+                held[g, :, h].astype(jnp.float32).reshape(inner * tile, HD).astype(jnp.bfloat16)
+            )
+
+    def send_across(n, d):
+        return pltpu.make_async_remote_copy(
+            src_ref=to_across.at[n, d], dst_ref=from_across.at[n, d],
+            send_sem=across_send.at[n, d], recv_sem=across_recv.at[n, d],
+            device_id=across[d], device_id_type=MESH,
+        )
+
+    @pl.loop(0, chunks)
+    def _(n):
+        w_copy(n).wait()
+        own[n] = jnp.dot(flat[...], w_here[n], preferred_element_type=jnp.float32).reshape(
+            inner, part, cw
+        )
+        for d in range(inner - 1):
+            to_across[n, d] = own[n, lax.rem(gy + d + 1, inner)].astype(jnp.bfloat16)
+            send_across(n, d).start()
+
+    @pl.loop(0, chunks)
+    def _(n):
+        for d in range(inner - 1):
+            send_across(n, d).wait()
+        for j in range(cw // HD):
+            columns = slice(j * HD, (j + 1) * HD)
+            total = own[n, gy, :, columns]
+            for d in range(inner - 1):
+                total = total + from_across[n, d, :, columns].astype(jnp.float32)
+            for q in range(groups):
+                for s in range(STEPS):
+                    piece[s, q * rows : (q + 1) * rows, :] = total[
+                        q * tile + s * rows : q * tile + (s + 1) * rows
+                    ]
+            place = pl.ds(pl.multiple_of(n * cw + j * HD, HD), HD)
+            out_first[:, place] = piece[0].astype(jnp.bfloat16)
+            out_second[:, place] = piece[1].astype(jnp.bfloat16)
+
+    for d in range(inner):
+        if d > 0:
+            send_z(d - 1).wait_send()
+        for e in range(pairs - 1):
+            send_along(d, e).wait_send()
+        for e in range(pairs):
+            share(d, e).wait_send()
+
+
+def finish(heads, w, outer, inner, rows):
+    count = heads.shape[1]
     depth, columns = w.shape
-    width = min(256, columns)
+    chunks = columns // min(512, columns)
+    cw = columns // chunks
+    pairs = outer // 2
+    tile = STEPS * rows
+    total = outer * inner * tile
+    part = total // inner
+    dims = (outer, inner, rows, chunks)
+    dma = pltpu.SemaphoreType.DMA
+    vmem = pl.BlockSpec(memory_space=pltpu.VMEM)
+    f32, b16 = jnp.float32, jnp.bfloat16
+    shape = jax.ShapeDtypeStruct((part // STEPS, columns), b16)
     return pl.pallas_call(
-        out_kernel,
-        grid=(columns // width,),
-        in_specs=[
-            pl.BlockSpec(heads.shape, lambda n: (0, 0, 0, 0, 0)),
-            pl.BlockSpec((depth, width), lambda n: (0, n)),
+        functools.partial(finish_kernel, dims),
+        in_specs=[vmem, pl.BlockSpec(memory_space=pl.ANY)],
+        out_specs=(vmem, vmem),
+        out_shape=(shape, shape),
+        scratch_shapes=[
+            pltpu.VMEM((outer, inner, count, tile, HD), b16),
+            pltpu.VMEM((total, depth), b16),
+            pltpu.VMEM((chunks, depth, cw), b16),
+            pltpu.VMEM((chunks, inner, part, cw), f32),
+            pltpu.VMEM((chunks, inner - 1, part, cw), b16),
+            pltpu.VMEM((chunks, inner - 1, part, cw), b16),
+            pltpu.VMEM((STEPS, part // STEPS, HD), f32),
+            dma((chunks,)),
+            dma((inner - 1,)), dma((inner - 1,)),
+            dma,
+            dma((inner, pairs - 1)), dma((inner, pairs - 1)),
+            dma((inner, pairs)), dma((inner, pairs)),
+            dma((chunks, inner - 1)), dma((chunks, inner - 1)),
         ],
-        out_specs=pl.BlockSpec((rows, width), lambda n: (0, n)),
-        out_shape=jax.ShapeDtypeStruct((rows, columns), jnp.float32),
-        scratch_shapes=[pltpu.VMEM((rows, depth), jnp.bfloat16)],
-        compiler_params=pltpu.CompilerParams(vmem_limit_bytes=VMEM_LIMIT),
+        compiler_params=pltpu.CompilerParams(
+            collective_id=1, has_side_effects=True, vmem_limit_bytes=VMEM_LIMIT
+        ),
+        name="finish",
     )(heads, w)
 
 
@@ -210,13 +491,9 @@
     outer, inner = lax.axis_size("gx"), lax.axis_size("gy")
     rows = lengths.shape[0]
     tile = STEPS * rows
-    depth = x_first.shape[1]
-    width = depth * outer
+    width = x_first.shape[1] * outer
     heads_here = w_qkv.shape[1] // HD
 
-    stacked = jnp.stack(
-        [x.reshape(outer * inner, rows, depth) for x in (x_first, x_second)], axis=1
-    ).reshape(outer * inner * tile, depth)
     half = HD // 2
     freq = rotary_base ** (-(jnp.arange(half, dtype=jnp.float32) * 2.0 / HD))
     position = jnp.concatenate([lengths + s for s in range(STEPS)])
@@ -224,21 +501,11 @@
     cosine = jnp.tile(jnp.cos(angle), (1, 2))
     sine = jnp.concatenate([-jnp.sin(angle), jnp.sin(angle)], axis=1)
 
-    partial_sum = qkv_partial(stacked, norm_gain[None], w_qkv, outer, inner)
-    summed = lax.psum_scatter(partial_sum, "gx", scatter_dimension=0, tiled=True)[0]
-    squares = summed[:, heads_here : heads_here + 1]
-    joined = (summed[:, :heads_here] * lax.rsqrt(squares / width + norm_eps)).astype(jnp.bfloat16)
-    joined = lax.all_to_all(joined, "gy", split_axis=0, concat_axis=0, tiled=True)
+    joined = project(x_first, x_second, norm_gain[None], w_qkv, outer, inner, rows, width)
     joined = joined.reshape(inner * heads_here, tile, HD)
-
     heads = attend(joined, cosine, sine, cache_keys, cache_values, lengths)
     heads = heads.reshape(inner, heads.shape[0] // inner, tile, HD)
-    heads = lax.all_to_all(heads, "gy", split_axis=0, concat_axis=0, tiled=True)
-    heads = lax.all_gather(heads, "gx", axis=0, tiled=False)
-    partial_out = out_partial(heads, w_out)
-    done = lax.psum_scatter(partial_out, "gy", scatter_dimension=0, tiled=True)
-    done = done.astype(jnp.bfloat16).reshape(-1, STEPS, rows, partial_out.shape[1])
-    return tuple(done[:, s].reshape(-1, partial_out.shape[1]) for s in range(STEPS))
+    return finish(heads, w_out, outer, inner, rows)
 
 
 def solution(mesh):

time: 225 us -> 95.6 us (0.42)
  waiting for transfers between devices: 136 us -> 0 us
  Pallas kernels: 45.2 us -> 86.6 us
  between operations: 13.8 us -> 0.65 us
  blocking collectives: 11.3 us -> 0 us
  starting transfers between devices: 4.69 us -> 0 us
  other arithmetic: 5.18 us -> 2.18 us
    reduce_scatter x2 -> x0, waiting for transfers between devices: 102 us -> none  [the longest x1 57.9 us: body(): lax.psum_scatter(partial_sum, 'gx', scatter_dimension=0, tiled=True)[0]]
    pallas_call x2, Pallas kernels: 31.4 us -> 72.8 us  [the longest x1 42.3 us: finish(): pl.pallas_call(functools.partial(finish_kernel, dims), in_specs=[vmem, pl...]
    all_gather x1 -> x0, waiting for transfers between devices: 26.3 us -> none  [body(): heads = lax.all_gather(heads, 'gx', axis=0, tiled=False)]
    all_to_all x1 -> x0, blocking collectives: 11.3 us -> none  [body(): heads = lax.all_to_all(heads, 'gy', split_axis=0, concat_axis=0, tiled=True)]
    all_to_all x1 -> x0, waiting for transfers between devices: 8.08 us -> none  [body(): lax.all_to_all(joined, 'gy', split_axis=0, concat_axis=0, tiled=True)]
    all_to_all x1 -> x0, starting transfers between devices: 4.61 us -> none  [body(): lax.all_to_all(joined, 'gy', split_axis=0, concat_axis=0, tiled=True)]
    another operation x4 -> x0, local copies, waits for them, and re-layouts: 3.85 us -> none  [the longest x2 2.48 us: body(): jnp.stack([x.reshape(outer * inner, rows, depth) for x in (x_first, x_sec...]
    convert_element_type x2 -> x0, other arithmetic: 2.9 us -> none  [the longest x1 1.83 us: body(): (summed[:, :heads_here] * lax.rsqrt(squares / width + norm_eps)).astype(j...]
  transfers between devices with their start and end apart: 4 -> 0, of which waited for: 4 -> 0; matrix products, arithmetic and copies ran while one was open for 1% -> 0% of each run, Pallas kernels for 0% -> 0%
where the time goes in v1:
time: 95.6 us; the launch traced here: 94.6 us
  Pallas kernels  86.6 us (91%)
  local copies, waits for them, and re-layouts  5.11 us (5%)
  other arithmetic  2.18 us (2%)
    pallas_call x1, Pallas kernels, finish(): pl.pallas_call(functools.partial(finish_kernel, dims), in_specs=[vmem, pl...  42.3 us
    pallas_call x1, Pallas kernels, project(): pl.pallas_call(functools.partial(project_kernel, dims), in_specs=[vmem, v...  30.6 us
    pallas_call x1, Pallas kernels, attend(): pl.pallas_call(functools.partial(attend_kernel, groups, size, rows), grid...  13.8 us
    unnamed x2, local copies, waits for them, and re-layouts  3.14 us

profile of v1, /device:TPU:0, one launch (start us, length us, event | category | flops | bytes accessed | tf_op | source)
XLA Modules:
  0.0 94.6 jit_solution(4643578079435726356)
XLA Ops:
  0.6 0.7 broadcast_add_fusion
  1.3 0.7 add_convert_fusion
  2.0 1.3 %broadcast_in_dim.2.gain = bf16[1,2048]{1,0:T(2,128)(2,1)} reshape(bf16[2048]{0:T(1024)(128)(2,1)} %param.10) | data formatting | bytes 8192 | tf_op jit(solution)/shard_map/broadcast_in_dim | solution.py:504
  3.3 0.1 fusion
  3.4 0.7 pad_maximum_fusion.sin_ref
  4.1 0.7 tile.10.cos_ref
  4.8 30.6 %project.1 = bf16[4,36,8,128]{3,2,1,0:T(8,128)(2,1)} custom-call(bf16[128,2048]{1,0:T(8,128)(2,1)} %x_first.1, bf16[128,2048]{1,0:T(8,128)(2,1)} %x_second.1, bf16[1,2048]{1,0:T(2,128)(2,1)} %broadcast_in_dim.2.gain, bf16[2048,4608]{1,0:T(8,128)(2,1)} %w.2), custom_call_target="tpu_custom_call" | custom-call | tf_op jit(solution)/shard_map/project/pallas_call | solution.py:189
  35.4 13.8 %shard_map.95 = bf16[128,8,128]{2,1,0:T(8,128)(2,1)} custom-call(s32[4]{0:T(128)} %lengths_ref.1, bf16[144,8,128]{2,1,0:T(8,128)(2,1)} %bitcast.2, f32[8,128]{1,0:T(8,128)} %tile.10.cos_ref, f32[8,128]{1,0:T(8,128)} %pad_maximum_fusion.sin_ref, bf16[4,768,1024]{2,1,0:T(8,128)(2,1)} %keys_ref.1, bf16[4,768,1024]{2,1,0:T(8,128)(2,1)} %values_ref.1), custom_call_target="tpu_custom_call" | custom-call | tf_op jit(solution)/shard_map/pallas_call | solution.py:308
  49.2 42.3 %finish.1 = (bf16[32,2048]{1,0:T(8,128)(2,1)}, bf16[32,2048]{1,0:T(8,128)(2,1)}) custom-call(bf16[4,32,8,128]{3,2,1,0:T(8,128)(2,1)} %bitcast.3, bf16[4096,2048]{1,0:T(8,128)(2,1)} %w.3), custom_call_target="tpu_custom_call" | custom-call | tf_op jit(solution)/shard_map/finish/pallas_call | solution.py:463
  91.4 1.6 %copy.12 = bf16[32,2048]{1,0:T(8,128)(2,1)} copy(bf16[32,2048]{1,0:T(8,128)(2,1)} %get-tuple-element.7) | data formatting | bytes 262144
  93.0 1.6 %copy.13 = bf16[32,2048]{1,0:T(8,128)(2,1)} copy(bf16[32,2048]{1,0:T(8,128)(2,1)} %get-tuple-element.8) | data formatting | bytes 262144
  (2 shorter events, 0.0 us)

commit v2 on v0

v2 whole, which is shorter than its diff:
```python
import functools
import math

import jax
import jax.numpy as jnp
import numpy as np
from jax import lax
from jax.experimental import pallas as pl
from jax.experimental.pallas import tpu as pltpu
from jax.sharding import PartitionSpec as P

HD = 128
norm_eps = 1e-05
rotary_base = 500000.0
STEPS = 2
BLOCK = 256
VMEM_LIMIT = 60 * 1024 * 1024
MESH = pl.DeviceIdType.MESH


def signal_peers(peers):
    barrier = pltpu.get_barrier_semaphore()
    for peer in peers:
        pl.semaphore_signal(barrier, inc=1, device_id=peer, device_id_type=MESH)
    pl.semaphore_wait(barrier, len(peers))


def remote(src, dst, send, recv, device):
    return pltpu.make_async_remote_copy(
        src_ref=src, dst_ref=dst, send_sem=send, recv_sem=recv,
        device_id=device, device_id_type=MESH,
    )


def block_kernel(
    dims, lengths, x_first, x_second, gain, freq, w_in, w_out, keys, values, result,
    x_here, k_here, v_here, weights, scaled, prod, from_other, to_along, from_along,
    sq, sq_other, sq_to, sq_along, mixed, to_across, joined,
    turned, mix, to_rows, held, flat, own, to_sum, from_sum, piece,
    x_sem, kv_sem, in_sem, out_sem, pair_send, pair_recv, along_send, along_recv,
    across_send, across_recv, sq_send, sq_recv, sqa_send, sqa_recv, own_sem,
    rows_send, rows_recv, keep_sem, gather_send, gather_recv, share_send, share_recv,
    sum_send, sum_recv,
):
    outer, inner, rows, width, groups, size, chunk_heads, chunks = dims
    gx, gy = lax.axis_index("gx"), lax.axis_index("gy")
    pairs = outer // 2
    pair, side = gx // 2, lax.rem(gx, 2)
    other = (gx + 1 - 2 * side, gy)
    along = [(2 * lax.rem(pair + d, pairs) + side, gy) for d in range(1, pairs)]
    across = [(gx, lax.rem(gy + d, inner)) for d in range(1, inner)]
    cw = chunk_heads * HD
    per_chunk = cw // BLOCK
    block = inner * rows
    here = STEPS * block
    tile = STEPS * rows
    per = size + 2
    chunks_each = chunks // groups
    slots = k_here.shape[1]
    depth = scaled.shape[1]
    out_blocks = own.shape[0]
    pieces = flat.shape[0]
    pieces_each = pieces // groups
    heads_piece = depth // HD
    part = own.shape[2]
    scale = 1.0 / math.sqrt(HD)

    x_copies = [
        pltpu.make_async_copy(x, x_here.at[s], x_sem.at[s])
        for s, x in enumerate((x_first, x_second))
    ]

    def in_copy(b):
        return pltpu.make_async_copy(
            w_in.at[:, pl.ds(pl.multiple_of(b * BLOCK, BLOCK), BLOCK)], weights.at[b], in_sem.at[b]
        )

    def out_copy(n, p):
        return pltpu.make_async_copy(
            w_out.at[
                pl.ds(p * depth, depth), pl.ds(pl.multiple_of(n * BLOCK, BLOCK), BLOCK)
            ],
            weights.at[n * pieces + p],
            out_sem.at[n, p],
        )

    kv_copies = [
        pltpu.make_async_copy(keys, k_here, kv_sem.at[0]),
        pltpu.make_async_copy(values, v_here, kv_sem.at[1]),
    ]

    def send_sq():
        return remote(sq.at[:, 1 - side], sq_other, sq_send, sq_recv, other)

    def send_sq_along(d):
        return remote(sq_to.at[d], sq_along.at[d], sqa_send.at[d], sqa_recv.at[d], along[d])

    def send_pair(n):
        return remote(
            prod.at[n, :, 1 - side], from_other.at[n], pair_send.at[n], pair_recv.at[n], other
        )

    def send_along(n, d):
        return remote(
            to_along.at[n, d], from_along.at[n, d],
            along_send.at[n, d], along_recv.at[n, d], along[d],
        )

    def columns_of(n):
        return pl.ds(n * chunk_heads, chunk_heads)

    def send_across(n, d):
        return remote(
            to_across.at[n, lax.rem(gy + d + 1, inner)], joined.at[gy, columns_of(n)],
            across_send.at[n, d], across_recv.at[n, d], across[d],
        )

    def keep_own(n):
        return pltpu.make_async_copy(
            to_across.at[n, gy], joined.at[gy, columns_of(n)], own_sem.at[n]
        )

    def source(d):
        return lax.rem(gy + inner - d, inner)

    def send_rows(j, d):
        return remote(
            to_rows.at[j, d], held.at[j, gx, gy], rows_send.at[j, d], rows_recv.at[j, d], across[d]
        )

    def keep_rows(j):
        return pltpu.make_async_copy(
            to_rows.at[j, inner - 1], held.at[j, gx, gy], keep_sem.at[j]
        )

    def gather(j, d, e):
        ref = held.at[j, gx, source(d)]
        return remote(ref, ref, gather_send.at[j, d, e], gather_recv.at[j, d, e], along[e])

    def share(j, d, e):
        ref = held.at[j, 2 * lax.rem(pair + pairs - e, pairs) + side, source(d)]
        return remote(ref, ref, share_send.at[j, d, e], share_recv.at[j, d, e], other)

    def send_sum(n, d):
        return remote(
            to_sum.at[n, d], from_sum.at[n, d], sum_send.at[n, d], sum_recv.at[n, d], across[d]
        )

    for copy in x_copies:
        copy.start()

    @pl.loop(0, chunks * per_chunk)
    def _(b):
        in_copy(b).start()

    for copy in kv_copies:
        copy.start()
    signal_peers([other] + along + across)

    wide_gain = gain[...].astype(jnp.float32).reshape(1, depth)
    for s in range(STEPS):
        x_copies[s].wait()

        @pl.loop(0, outer)
        def _(g):
            wide = x_here[s, pl.ds(pl.multiple_of(g * block, block), block), :].astype(jnp.float32)
            row = pl.multiple_of(g * here + s * block, block)
            scaled[pl.ds(row, block), :] = (wide * wide_gain).astype(jnp.bfloat16)
            total = jnp.sum(wide * wide, axis=1, keepdims=True)
            sq[g // 2, lax.rem(g, 2), s * block : (s + 1) * block, :] = jnp.broadcast_to(
                total, (block, HD)
            )

    send_sq().start()

    def pass_on(n):
        send_pair(n).wait()
        for d in range(pairs - 1):
            there = lax.rem(pair + d + 1, pairs)
            to_along[n, d] = (prod[n, there, side] + from_other[n, there]).astype(jnp.bfloat16)
            send_along(n, d).start()

    @pl.loop(0, chunks)
    def _(n):
        for c in range(per_chunk):
            b = n * per_chunk + c
            in_copy(b).wait()
            product = jnp.dot(scaled[...], weights[b], preferred_element_type=jnp.float32)
            prod[n, :, :, :, c * BLOCK : (c + 1) * BLOCK] = product.reshape(pairs, 2, here, BLOCK)
        send_pair(n).start()

        @pl.when(n == 0)
        def _():
            send_sq().wait()
            for d in range(pairs - 1):
                there = lax.rem(pair + d + 1, pairs)
                sq_to[d] = sq[there, side] + sq_other[there]
                send_sq_along(d).start()

        @pl.when(n > 0)
        def _():
            pass_on(n - 1)

    pass_on(chunks - 1)

    @pl.loop(0, out_blocks)
    def _(n):
        for p in range(pieces):
            out_copy(n, p).start()

    squares = sq[pair, side] + sq_other[pair]
    for d in range(pairs - 1):
        send_sq_along(d).wait()
        squares = squares + sq_along[d]
    sq[0, 0] = lax.rsqrt(squares / width + norm_eps)

    def settle(n):
        for d in range(pairs - 1):
            send_along(n, d).wait()
        for h in range(chunk_heads):
            columns = slice(h * HD, (h + 1) * HD)
            total = prod[n, pair, side, :, columns] + from_other[n, pair, :, columns]
            for d in range(pairs - 1):
                total = total + from_along[n, d, :, columns].astype(jnp.float32)
            total = total * sq[0, 0]
            for s in range(STEPS):
                for z in range(inner):
                    mixed[h, z * tile + s * rows : z * tile + (s + 1) * rows, :] = total[
                        s * block + z * rows : s * block + (z + 1) * rows
                    ]
            for z in range(inner):
                to_across[n, z, h] = mixed[h, z * tile : (z + 1) * tile, :].astype(jnp.bfloat16)
        for d in range(inner - 1):
            send_across(n, d).start()
        keep_own(n).start()

    @pl.loop(0, chunks_each)
    def _(n):
        settle(n)

    index = lax.broadcasted_iota(jnp.int32, (tile, HD), 0)
    lane = lax.broadcasted_iota(jnp.int32, (tile, HD), 1)
    position = jnp.zeros((tile, HD), jnp.float32)
    for s in range(STEPS):
        for i in range(rows):
            position = jnp.where(
                index == s * rows + i, (lengths[i] + s).astype(jnp.float32), position
            )
    angle = position * freq[...]
    cosine = jnp.cos(angle)
    sine = jnp.where(lane < HD // 2, -jnp.sin(angle), jnp.sin(angle))
    late = lax.broadcasted_iota(jnp.int32, (STEPS * size, 1), 0) >= size

    def forward(j, d):
        for e in range(pairs - 1):
            gather(j, d, e).start()
        share(j, d, 0).start()

    for copy in kv_copies:
        copy.wait()

    for j in range(groups):

        @pl.loop(j * chunks_each, (j + 1) * chunks_each)
        def _(n):
            keep_own(n).wait()
            for d in range(inner - 1):
                send_across(n, d).wait()

        @pl.loop(0, inner)
        def _(d):
            there = lax.rem(gy + d + 1, inner)
            turn = joined[there, j * per : j * per + size + 1].astype(jnp.float32)
            turn = turn * cosine[None] + pltpu.roll(turn, HD // 2, 2) * sine[None]
            turn = turn.astype(jnp.bfloat16).astype(jnp.float32)
            turned[: (size + 1) * tile] = turn.reshape((size + 1) * tile, HD)
            turned[(size + 1) * tile :] = joined[there, j * per + size + 1].astype(jnp.float32)
            place = pl.ds(pl.multiple_of((there * groups + j) * HD, HD), HD)
            for i in range(rows):
                valid = lax.broadcasted_iota(jnp.int32, (1, slots), 1) < lengths[i]
                query = jnp.concatenate(
                    [turned[pl.ds(s * rows + i, size, stride=tile), :] for s in range(STEPS)],
                    axis=0,
                )
                new_keys = [
                    turned[size * tile + s * rows + i : size * tile + s * rows + i + 1, :]
                    for s in range(STEPS)
                ]
                first = (size + 1) * tile
                new_values = [
                    turned[first + s * rows + i : first + s * rows + i + 1, :]
                    for s in range(STEPS)
                ]
                scores = (
                    lax.dot_general(
                        query.astype(jnp.bfloat16),
                        k_here[i, :, place],
                        (((1,), (1,)), ((), ())),
                        preferred_element_type=jnp.float32,
                    )
                    * scale
                )
                scores = jnp.where(valid, scores, -jnp.inf)
                extra_one = jnp.sum(query * new_keys[0], axis=1, keepdims=True) * scale
                extra_two = jnp.sum(query * new_keys[1], axis=1, keepdims=True) * scale
                extra_two = jnp.where(late, extra_two, -jnp.inf)
                top = jnp.maximum(
                    jnp.max(scores, axis=1, keepdims=True), jnp.maximum(extra_one, extra_two)
                )
                soft = jnp.exp(scores - top)
                soft_one = jnp.exp(extra_one - top)
                soft_two = jnp.exp(extra_two - top)
                total = jnp.sum(soft, axis=1, keepdims=True) + soft_one + soft_two
                blend = jnp.dot(
                    soft.astype(jnp.bfloat16),
                    v_here[i, :, place],
                    preferred_element_type=jnp.float32,
                )
                blend = (
                    blend
                    + soft_one.astype(jnp.bfloat16).astype(jnp.float32) * new_values[0]
                    + soft_two.astype(jnp.bfloat16).astype(jnp.float32) * new_values[1]
                )
                blend = blend / total
                for s in range(STEPS):
                    mix[pl.ds(s * rows + i, size, stride=tile), :] = blend[
                        s * size : (s + 1) * size
                    ]
            to_rows[j, d] = mix[...].reshape(size, tile, HD).astype(jnp.bfloat16)

            for c in range(inner - 1):

                @pl.when(d == c)
                def _():
                    send_rows(j, c).start()

            if j + 1 < groups:
                for c in range(chunks_each):

                    @pl.when(d == min(c, inner - 1))
                    def _():
                        settle((j + 1) * chunks_each + c)

            if j > 0:

                @pl.when(d == 0)
                def _():
                    keep_rows(j - 1).wait()
                    forward(j - 1, 0)

                for c in range(1, inner):

                    @pl.when(d == c)
                    def _():
                        send_rows(j - 1, c - 1).wait_recv()
                        forward(j - 1, c)

        keep_rows(j).start()

    last = groups - 1

    def fill(j):
        @pl.loop(0, outer)
        def _(g):
            row = pl.multiple_of(g * inner * tile, inner * tile)
            for h in range(size):
                p = j * pieces_each + h // heads_piece
                column = (h % heads_piece) * HD
                flat[p, pl.ds(row, inner * tile), column : column + HD] = (
                    held[j, g, :, h].astype(jnp.float32).reshape(inner * tile, HD)
                    .astype(jnp.bfloat16)
                )

    def share_arrived(j):
        for d in range(inner):
            for e in range(pairs - 1):
                gather(j, d, e).wait_recv()
                share(j, d, e + 1).start()

    def take_shared(j):
        for d in range(inner):
            for e in range(pairs):
                share(j, d, e).wait_recv()

    for j in range(groups - 1):
        share_arrived(j)
    keep_rows(last).wait()
    forward(last, 0)
    for d in range(1, inner):
        send_rows(last, d - 1).wait_recv()
        forward(last, d)

    for j in range(groups - 1):
        take_shared(j)
        fill(j)

        @pl.loop(0, out_blocks)
        def _(n):
            for p in range(j * pieces_each, (j + 1) * pieces_each):
                out_copy(n, p).wait()
                product = jnp.dot(
                    flat[p], weights[n * pieces + p], preferred_element_type=jnp.float32
                ).reshape(inner, part, BLOCK)
                own[n] = product if p == 0 else own[n] + product

    share_arrived(last)
    take_shared(last)
    fill(last)

    @pl.loop(0, out_blocks)
    def _(n):
        total = None if last == 0 else own[n]
        for p in range(last * pieces_each, pieces):
            out_copy(n, p).wait()
            product = jnp.dot(
                flat[p], weights[n * pieces + p], preferred_element_type=jnp.float32
            ).reshape(inner, part, BLOCK)
            total = product if total is None else total + product
        own[n] = total
        for d in range(inner - 1):
            to_sum[n, d] = own[n, lax.rem(gy + d + 1, inner)].astype(jnp.bfloat16)
            send_sum(n, d).start()

    @pl.loop(0, out_blocks)
    def _(n):
        for d in range(inner - 1):
            send_sum(n, d).wait()
        for c in range(BLOCK // HD):
            columns = slice(c * HD, (c + 1) * HD)
            total = own[n, gy, :, columns]
            for d in range(inner - 1):
                total = total + from_sum[n, d, :, columns].astype(jnp.float32)
            for q in range(part // tile):
                for s in range(STEPS):
                    piece[s, q * rows : (q + 1) * rows, :] = total[
                        q * tile + s * rows : q * tile + (s + 1) * rows
                    ]
            place = pl.ds(pl.multiple_of(n * BLOCK + c * HD, HD), HD)
            for s in range(STEPS):
                result[s, :, place] = piece[s].astype(jnp.bfloat16)

    for j in range(groups):
        for d in range(inner):
            if d > 0:
                send_rows(j, d - 1).wait_send()
            for e in range(pairs - 1):
                gather(j, d, e).wait_send()
            for e in range(pairs):
                share(j, d, e).wait_send()


def body(x_first, x_second, norm_gain, w_qkv, w_out, cache_keys, cache_values, lengths):
    outer, inner = lax.axis_size("gx"), lax.axis_size("gy")
    rows, slots, kv_width = cache_keys.shape
    depth, in_columns = w_qkv.shape
    out_depth, out_columns = w_out.shape
    width = depth * outer
    heads = in_columns // HD
    groups = kv_width // HD // inner
    size = heads // groups - 2
    chunk_heads = 6
    chunks = heads // chunk_heads
    cw = chunk_heads * HD
    pairs = outer // 2
    here = STEPS * inner * rows
    tile = STEPS * rows
    total = outer * here
    part = total // inner
    out_blocks = out_columns // BLOCK
    pieces = out_depth // depth
    dims = (outer, inner, rows, width, groups, size, chunk_heads, chunks)

    half = HD // 2
    freq = rotary_base ** (-(np.arange(half, dtype=np.float64) * 2.0 / HD))
    freq = jnp.asarray(np.tile(freq, 2)[None], jnp.float32)

    dma = pltpu.SemaphoreType.DMA
    vmem = pl.BlockSpec(memory_space=pltpu.VMEM)
    away = pl.BlockSpec(memory_space=pl.ANY)
    f32, b16 = jnp.float32, jnp.bfloat16
    result = pl.pallas_call(
        functools.partial(block_kernel, dims),
        in_specs=[
            pl.BlockSpec(memory_space=pltpu.SMEM), away, away, vmem, vmem, away, away, away, away,
        ],
        out_specs=vmem,
        out_shape=jax.ShapeDtypeStruct((STEPS, part // STEPS, out_columns), b16),
        scratch_shapes=[
            pltpu.VMEM((STEPS, outer * inner * rows, depth), b16),
            pltpu.VMEM((rows, slots, kv_width), b16),
            pltpu.VMEM((rows, slots, kv_width), b16),
            pltpu.VMEM((max(in_columns // BLOCK, out_blocks * pieces), depth, BLOCK), b16),
            pltpu.VMEM((total, depth), b16),
            pltpu.VMEM((chunks, pairs, 2, here, cw), f32),
            pltpu.VMEM((chunks, pairs, here, cw), f32),
            pltpu.VMEM((chunks, pairs - 1, here, cw), b16),
            pltpu.VMEM((chunks, pairs - 1, here, cw), b16),
            pltpu.VMEM((pairs, 2, here, HD), f32),
            pltpu.VMEM((pairs, here, HD), f32),
            pltpu.VMEM((pairs - 1, here, HD), f32),
            pltpu.VMEM((pairs - 1, here, HD), f32),
            pltpu.VMEM((chunk_heads, here, HD), f32),
            pltpu.VMEM((chunks, inner, chunk_heads, tile, HD), b16),
            pltpu.VMEM((inner, heads, tile, HD), b16),
            pltpu.VMEM(((size + 2) * tile, HD), f32),
            pltpu.VMEM((size * tile, HD), f32),
            pltpu.VMEM((groups, inner, size, tile, HD), b16),
            pltpu.VMEM((groups, outer, inner, size, tile, HD), b16),
            pltpu.VMEM((pieces, total, depth), b16),
            pltpu.VMEM((out_blocks, inner, part, BLOCK), f32),
            pltpu.VMEM((out_blocks, inner - 1, part, BLOCK), b16),
            pltpu.VMEM((out_blocks, inner - 1, part, BLOCK), b16),
            pltpu.VMEM((STEPS, part // STEPS, HD), f32),
            dma((STEPS,)), dma((2,)), dma((in_columns // BLOCK,)), dma((out_blocks, pieces)),
            dma((chunks,)), dma((chunks,)),
            dma((chunks, pairs - 1)), dma((chunks, pairs - 1)),
            dma((chunks, inner - 1)), dma((chunks, inner - 1)),
            dma, dma, dma((pairs - 1,)), dma((pairs - 1,)), dma((chunks,)),
            dma((groups, inner - 1)), dma((groups, inner - 1)), dma((groups,)),
            dma((groups, inner, pairs - 1)), dma((groups, inner, pairs - 1)),
            dma((groups, inner, pairs)), dma((groups, inner, pairs)),
            dma((out_blocks, inner - 1)), dma((out_blocks, inner - 1)),
        ],
        compiler_params=pltpu.CompilerParams(
            collective_id=0, has_side_effects=True, vmem_limit_bytes=VMEM_LIMIT
        ),
        name="decode_block",
    )(lengths, x_first, x_second, norm_gain, freq, w_qkv, w_out, cache_keys, cache_values)
    return result[0], result[1]


def solution(mesh):
    in_specs = (
        P(None, "gx"),
        P(None, "gx"),
        P("gx"),
        P("gx", "gy"),
        P("gy", "gx"),
        P(("gx", "gy"), None, None),
        P(("gx", "gy"), None, None),
        P(("gx", "gy")),
    )
    out_specs = (P("gy", "gx"), P("gy", "gx"))
    return jax.shard_map(body, mesh=mesh, in_specs=in_specs, out_specs=out_specs, check_vma=False)
```

time: 225 us -> 82.7 us (0.37)
  waiting for transfers between devices: 136 us -> 0 us
  Pallas kernels: 45.2 us -> 80 us
  between operations: 13.8 us -> 0.64 us
  blocking collectives: 11.3 us -> 0 us
  local copies, waits for them, and re-layouts: 7.2 us -> 1.68 us
  other arithmetic: 5.18 us -> 0 us
  starting transfers between devices: 4.69 us -> 0 us
    reduce_scatter x2 -> x0, waiting for transfers between devices: 102 us -> none  [the longest x1 57.9 us: body(): lax.psum_scatter(partial_sum, 'gx', scatter_dimension=0, tiled=True)[0]]
    pallas_call x3 -> x1, Pallas kernels: 45.2 us -> 80 us  [body(): pl.pallas_call(functools.partial(block_kernel, dims), in_specs=[pl.BlockS...]
    all_gather x1 -> x0, waiting for transfers between devices: 26.3 us -> none  [body(): heads = lax.all_gather(heads, 'gx', axis=0, tiled=False)]
    all_to_all x1 -> x0, blocking collectives: 11.3 us -> none  [body(): heads = lax.all_to_all(heads, 'gy', split_axis=0, concat_axis=0, tiled=True)]
    all_to_all x1 -> x0, waiting for transfers between devices: 8.08 us -> none  [body(): lax.all_to_all(joined, 'gy', split_axis=0, concat_axis=0, tiled=True)]
    all_to_all x1 -> x0, starting transfers between devices: 4.61 us -> none  [body(): lax.all_to_all(joined, 'gy', split_axis=0, concat_axis=0, tiled=True)]
    another operation x6 -> x0, local copies, waits for them, and re-layouts: 4.53 us -> none  [the longest x2 2.48 us: body(): jnp.stack([x.reshape(outer * inner, rows, depth) for x in (x_first, x_sec...]
    convert_element_type x3 -> x0, other arithmetic: 2.97 us -> none  [the longest x1 1.83 us: body(): (summed[:, :heads_here] * lax.rsqrt(squares / width + norm_eps)).astype(j...]
  transfers between devices with their start and end apart: 4 -> 0, of which waited for: 4 -> 0; matrix products, arithmetic and copies ran while one was open for 1% -> 0% of each run, Pallas kernels for 0% -> 0%
where the time goes in v2:
time: 82.7 us; the launch traced here: 82.3 us
  Pallas kernels  80 us (97%)
  local copies, waits for them, and re-layouts  1.68 us (2%)
    pallas_call x1, Pallas kernels, body(): pl.pallas_call(functools.partial(block_kernel, dims), in_specs=[pl.BlockS...  80 us
    squeeze x1, local copies, waits for them, and re-layouts, body(): return (result[0], result[1])  1.68 us

profile of v2, /device:TPU:0, one launch (start us, length us, event | category | flops | bytes accessed | tf_op | source)
XLA Modules:
  0.0 82.3 jit_solution(667351593593208299)
XLA Ops:
  0.6 80.0 %decode_block.1 = bf16[2,32,2048]{2,1,0:T(8,128)(2,1)} custom-call(s32[4]{0:T(128)} %lengths.1, bf16[128,2048]{1,0:T(8,128)(2,1)} %x_first.1, bf16[128,2048]{1,0:T(8,128)(2,1)} %x_second.1, bf16[2048]{0:T(1024)(128)(2,1)} %gain.1, f32[1,128]{1,0:T(1,128)} %constant.2.clone.freq, bf16[2048,4608]{1,0:T(8,128)(2,1)} %w_in.1, bf16[4096,2048]{1,0:T(8,128)(2,1)} %w_out.1, ...), custom_call_target="tpu_custom_call" | custom-call | tf_op jit(solution)/shard_map/decode_block/pallas_call | solution.py:481
  80.6 1.7 %slice_bitcast_fusion = (bf16[32,2048]{1,0:T(8,128)(2,1)}, bf16[32,2048]{1,0:T(8,128)(2,1)}) fusion(bf16[2,32,2048]{2,1,0:T(8,128)(2,1)} %decode_block.1), kind=kLoop, calls=%fused_computation | loop fusion | bytes 524288 | tf_op jit(solution)/shard_map/squeeze | solution.py:529

commit v3 on v2

v3 whole, which is shorter than its diff:
```python
import functools
import math

import jax
import jax.numpy as jnp
import numpy as np
from jax import lax
from jax.experimental import pallas as pl
from jax.experimental.pallas import tpu as pltpu
from jax.sharding import PartitionSpec as P

HD = 128
norm_eps = 1e-05
rotary_base = 500000.0
STEPS = 2
HALVES = 2
SUB = 8
EXTRA = 16
VMEM_LIMIT = 62 * 1024 * 1024
MESH = pl.DeviceIdType.MESH


def remote(src, dst, send, recv, device):
    return pltpu.make_async_remote_copy(
        src_ref=src, dst_ref=dst, send_sem=send, recv_sem=recv,
        device_id=device, device_id_type=MESH,
    )


def block_kernel(
    dims, lengths, x_first, x_second, gain, freq, w_in, w_out, keys, values, result,
    x_here, k_here, v_here, weights, scaled, prod, from_other, to_along, from_along,
    sq, sq_other, sq_to, sq_along, mixed, to_across, joined,
    turned, spread, fresh, mix, to_rows, held, parted, flat, own, to_sum, from_sum, piece,
    x_sem, kv_sem, in_sem, out_sem, pair_send, pair_recv, along_send, along_recv,
    across_send, across_recv, sq_send, sq_recv, sqa_send, sqa_recv, own_sem,
    rows_send, rows_recv, keep_sem, gather_send, gather_recv, share_send, share_recv,
    sum_send, sum_recv,
):
    outer, inner, rows, width, groups, size, chunk_heads, chunks = dims
    gx, gy = lax.axis_index("gx"), lax.axis_index("gy")
    pairs = outer // 2
    pair, side = gx // 2, lax.rem(gx, 2)
    other = (gx + 1 - 2 * side, gy)
    along = [(2 * lax.rem(pair + d, pairs) + side, gy) for d in range(1, pairs)]
    across = [(gx, lax.rem(gy + d, inner)) for d in range(1, inner)]
    cw = chunk_heads * HD
    block = inner * rows
    here = STEPS * block
    half_rows = rows // HALVES
    tile = STEPS * half_rows
    per_tile = SUB // tile
    per = size + 2
    slots = k_here.shape[1] - EXTRA
    half = here // HALVES
    depth = scaled.shape[1]
    out_blocks = own.shape[1]
    pieces = flat.shape[1]
    part = own.shape[3]
    scale = 1.0 / math.sqrt(HD)

    x_copies = [
        pltpu.make_async_copy(x, x_here.at[s], x_sem.at[s])
        for s, x in enumerate((x_first, x_second))
    ]

    def in_copy(b):
        return pltpu.make_async_copy(
            w_in.at[:, pl.ds(pl.multiple_of(b * cw, cw), cw)], weights.at[b], in_sem.at[b]
        )

    def out_copy(n, p):
        return pltpu.make_async_copy(
            w_out.at[
                pl.ds(p * depth, depth), pl.ds(pl.multiple_of(n * cw, cw), cw)
            ],
            weights.at[n * pieces + p],
            out_sem.at[n, p],
        )

    kv_copies = [
        pltpu.make_async_copy(keys, k_here.at[:, pl.ds(0, slots)], kv_sem.at[0]),
        pltpu.make_async_copy(values, v_here.at[:, pl.ds(0, slots)], kv_sem.at[1]),
    ]

    def send_sq():
        return remote(sq.at[:, 1 - side], sq_other, sq_send, sq_recv, other)

    def send_sq_along(d):
        return remote(sq_to.at[d], sq_along.at[d], sqa_send.at[d], sqa_recv.at[d], along[d])

    def send_pair(n):
        return remote(
            prod.at[n, :, 1 - side], from_other.at[n], pair_send.at[n], pair_recv.at[n], other
        )

    def send_along(n, f, d):
        return remote(
            to_along.at[n, f, d], from_along.at[n, f, d],
            along_send.at[n, f, d], along_recv.at[n, f, d], along[d],
        )

    def send_across(n, f, d):
        return remote(
            to_across.at[n, f, lax.rem(gy + d + 1, inner)], joined.at[gy, n, f],
            across_send.at[n, f, d], across_recv.at[n, f, d], across[d],
        )

    def keep_own(n, f):
        return pltpu.make_async_copy(
            to_across.at[n, f, gy], joined.at[gy, n, f], own_sem.at[n, f]
        )

    def source(d):
        return lax.rem(gy + inner - d, inner)

    def send_rows(f, d):
        return remote(
            to_rows.at[f, d], held.at[f, gx, gy], rows_send.at[f, d], rows_recv.at[f, d], across[d]
        )

    def keep_rows(f):
        return pltpu.make_async_copy(
            to_rows.at[f, inner - 1], held.at[f, gx, gy], keep_sem.at[f]
        )

    def gather(f, d, e):
        ref = held.at[f, gx, source(d)]
        return remote(ref, ref, gather_send.at[f, d, e], gather_recv.at[f, d, e], along[e])

    def share(f, d, e):
        ref = held.at[f, 2 * lax.rem(pair + pairs - e, pairs) + side, source(d)]
        return remote(ref, ref, share_send.at[f, d, e], share_recv.at[f, d, e], other)

    def send_sum(f, n, d):
        return remote(
            to_sum.at[f, n, d], from_sum.at[f, n, d],
            sum_send.at[f, n, d], sum_recv.at[f, n, d], across[d],
        )

    for copy in x_copies:
        copy.start()

    @pl.loop(0, chunks)
    def _(b):
        in_copy(b).start()

    for copy in kv_copies:
        copy.start()

    barrier = pltpu.get_barrier_semaphore()
    peers = [other] + along + across
    for peer in peers:
        pl.semaphore_signal(barrier, inc=1, device_id=peer, device_id_type=MESH)

    to = lax.broadcasted_iota(jnp.int32, (here, here), 0)
    step = lax.rem(lax.div(to, half_rows), STEPS)
    member = lax.rem(lax.div(to, tile), inner)
    start = lax.div(to, half) * half_rows + lax.rem(to, half_rows)
    source_row = step * block + member * rows + start
    order = jnp.where(
        source_row == lax.broadcasted_iota(jnp.int32, (here, here), 1), 1.0, 0.0
    ).astype(jnp.bfloat16)
    wide_gain = gain[...].astype(jnp.float32).reshape(1, depth)
    for copy in x_copies:
        copy.wait()

    @pl.loop(0, outer)
    def _(g):
        parts = []
        for s in range(STEPS):
            wide = x_here[s, pl.ds(pl.multiple_of(g * block, block), block), :].astype(jnp.float32)
            parts.append((wide * wide_gain).astype(jnp.bfloat16))
            total = jnp.sum(wide * wide, axis=1, keepdims=True)
            sq[g // 2, lax.rem(g, 2), s * block : (s + 1) * block, :] = jnp.broadcast_to(
                total, (block, HD)
            )
        scaled[pl.ds(pl.multiple_of(g * here, here), here), :] = jnp.dot(
            order, jnp.concatenate(parts, axis=0), preferred_element_type=jnp.float32
        ).astype(jnp.bfloat16)

    pl.semaphore_wait(barrier, len(peers))
    send_sq().start()

    def pass_on(n):
        send_pair(n).wait()
        for d in range(pairs - 1):
            there = lax.rem(pair + d + 1, pairs)
            both = (prod[n, there, side] + from_other[n, there]).astype(jnp.bfloat16)
            for f in range(HALVES):
                to_along[n, f, d] = both[f * half : (f + 1) * half]
            send_along(n, 0, d).start()

    @pl.loop(0, chunks)
    def _(n):
        in_copy(n).wait()
        product = jnp.dot(scaled[...], weights[n], preferred_element_type=jnp.float32)
        prod[n] = product.reshape(pairs, 2, here, cw)
        send_pair(n).start()

        @pl.when(n == 0)
        def _():
            send_sq().wait()
            for d in range(pairs - 1):
                there = lax.rem(pair + d + 1, pairs)
                sq_to[d] = sq[there, side] + sq_other[there]
                send_sq_along(d).start()

        @pl.when(n > 0)
        def _():
            pass_on(n - 1)

    pass_on(chunks - 1)

    @pl.loop(0, chunks)
    def _(n):
        for f in range(1, HALVES):
            for d in range(pairs - 1):
                send_along(n, f, d).start()

    @pl.loop(0, out_blocks)
    def _(n):
        for p in range(pieces):
            out_copy(n, p).start()

    squares = sq[pair, side] + sq_other[pair]
    for d in range(pairs - 1):
        send_sq_along(d).wait()
        squares = squares + sq_along[d]
    factor = lax.rsqrt(squares / width + norm_eps)
    for f in range(HALVES):
        for z in range(inner):
            for s in range(STEPS):
                target = f * half + z * tile + s * half_rows
                row = s * block + z * rows + f * half_rows
                sq[0, 0, target : target + half_rows, :] = factor[row : row + half_rows]

    index = lax.rem(lax.broadcasted_iota(jnp.int32, (SUB, HD), 0), tile)
    lane = lax.broadcasted_iota(jnp.int32, (SUB, HD), 1)
    cosines, sines = [], []
    for f in range(HALVES):
        position = jnp.zeros((SUB, HD), jnp.float32)
        for s in range(STEPS):
            for i in range(half_rows):
                position = jnp.where(
                    index == s * half_rows + i,
                    (lengths[f * half_rows + i] + s).astype(jnp.float32),
                    position,
                )
        angle = position * freq[...]
        cosines.append(jnp.cos(angle))
        sines.append(jnp.where(lane < HD // 2, -jnp.sin(angle), jnp.sin(angle)))

    def settle(n, f):
        for d in range(pairs - 1):
            send_along(n, f, d).wait()
        span = slice(f * half, (f + 1) * half)
        for h in range(chunk_heads):
            columns = slice(h * HD, (h + 1) * HD)
            total = prod[n, pair, side, span, columns] + from_other[n, pair, span, columns]
            for d in range(pairs - 1):
                total = total + from_along[n, f, d, :, columns].astype(jnp.float32)
            total = total * sq[0, 0, span, :]
            for z in range(inner):
                mixed[z, h * tile : (h + 1) * tile, :] = total[z * tile : (z + 1) * tile]
        for z in range(inner):
            to_across[n, f, z] = (
                mixed[z].reshape(chunk_heads // per_tile, SUB, HD).astype(jnp.bfloat16)
            )
        for d in range(inner - 1):
            send_across(n, f, d).start()
        keep_own(n, f).start()

    early = chunks // 2

    @pl.loop(0, chunks)
    def _(n):
        settle(n, 0)

    @pl.loop(0, early)
    def _(n):
        settle(n, 1)

    upper = lax.broadcasted_iota(jnp.int32, (SUB, HD), 0) < tile
    queries = size // per_tile
    kv_heads = inner * groups
    columns = kv_heads * STEPS * size
    slot = lax.broadcasted_iota(jnp.int32, (slots + EXTRA, columns), 0)
    column = lax.broadcasted_iota(jnp.int32, (1, columns), 1)
    newest = jnp.where(lax.rem(column, STEPS * size) >= size, slots + 1, slots)

    def forward(f, d):
        for e in range(pairs - 1):
            gather(f, d, e).start()
        share(f, d, 0).start()

    def forward_all(f):
        keep_rows(f).wait()
        forward(f, 0)
        for d in range(1, inner):
            send_rows(f, d - 1).wait_recv()
            forward(f, d)

    fresh[...] = jnp.zeros_like(fresh)

    @pl.loop(0, half_rows)
    def _(i):
        spread[i] = jnp.zeros(spread.shape[1:], jnp.bfloat16)

    for copy in kv_copies:
        copy.wait()

    for f in range(HALVES):

        @pl.loop(0, chunks)
        def _(n):
            if f > 0:

                @pl.when(n >= early)
                def _():
                    settle(n, f)

        @pl.loop(0, chunks)
        def _(n):
            keep_own(n, f).wait()
            for d in range(inner - 1):
                send_across(n, f, d).wait()

        if f > 0:
            forward_all(f - 1)

        @pl.loop(0, inner)
        def _(y):
            here_now = joined[y, :, f].reshape(groups * per * tile // SUB, SUB, HD)
            for j in range(groups):
                k = y * groups + j
                turn = here_now[j * per * tile // SUB : (j + 1) * per * tile // SUB]
                turn = turn.astype(jnp.float32)
                turned_now = turn * cosines[f][None] + pltpu.roll(turn, HD // 2, 2) * sines[f][None]
                turned_now = turned_now.astype(jnp.bfloat16).astype(jnp.float32)
                turned[j, : size * tile] = turned_now[:queries].reshape(size * tile, HD)
                turned[j, size * tile :] = jnp.where(upper, turned_now[queries], turn[queries])
                place = pl.ds(pl.multiple_of(k * HD, HD), HD)
                band = pl.ds(pl.multiple_of(k * STEPS * size, STEPS * size), STEPS * size)
                for i in range(half_rows):
                    query = jnp.concatenate(
                        [
                            turned[j, pl.ds(s * half_rows + i, size, stride=tile), :]
                            for s in range(STEPS)
                        ],
                        axis=0,
                    )
                    spread[i, band, place] = query.astype(jnp.bfloat16)
                    for s in range(STEPS):
                        for c in range(2):
                            row = (size + c) * tile + s * half_rows + i
                            fresh[i, c, s : s + 1, place] = turned[j, row : row + 1, :]

        for i in range(half_rows):
            row = f * half_rows + i
            k_here[row, slots:, :] = fresh[i, 0].astype(jnp.bfloat16)
            v_here[row, slots:, :] = fresh[i, 1].astype(jnp.bfloat16)
            scores = (
                lax.dot_general(
                    k_here[row],
                    spread[i],
                    (((1,), (1,)), ((), ())),
                    preferred_element_type=jnp.float32,
                )
                * scale
            )
            valid = (slot < lengths[row]) | ((slot >= slots) & (slot <= newest))
            scores = jnp.where(valid, scores, -jnp.inf)
            soft = jnp.exp(scores - jnp.max(scores, axis=0, keepdims=True))
            total = jnp.sum(soft, axis=0, keepdims=True)
            total = jnp.broadcast_to(total, (SUB, columns)).T
            soft = soft.astype(jnp.bfloat16).T
            for k in range(kv_heads):
                band = slice(k * STEPS * size, (k + 1) * STEPS * size)
                blend = jnp.dot(
                    soft[band],
                    v_here[row, :, k * HD : (k + 1) * HD],
                    preferred_element_type=jnp.float32,
                )
                blend = blend / total[band, 0:1]
                for s in range(STEPS):
                    mix[k, pl.ds(s * half_rows + i, size, stride=tile), :] = blend[
                        s * size : (s + 1) * size
                    ]

        for d in range(inner):
            there = lax.rem(gy + d + 1, inner)
            for j in range(groups):
                to_rows[f, d, j] = (
                    mix[there * groups + j].reshape(queries, SUB, HD).astype(jnp.bfloat16)
                )
            if d < inner - 1:
                send_rows(f, d).start()
        keep_rows(f).start()

    heads_piece = depth // HD
    span = inner * tile

    def pass_side(f):
        for d in range(inner):
            for e in range(pairs - 1):
                gather(f, d, e).wait_recv()
                share(f, d, e + 1).start()

    def bring(f):
        for d in range(inner):
            for e in range(pairs):
                share(f, d, e).wait_recv()

        @pl.loop(0, outer)
        def _(g):
            place = pl.ds(pl.multiple_of(g * span, span), span)
            for j in range(groups):
                for q in range(queries):
                    both = held[f, g, :, j, q].astype(jnp.float32)
                    for t in range(per_tile):
                        for z in range(inner):
                            parted[q, t, z * tile : (z + 1) * tile, :] = both[
                                z, t * tile : (t + 1) * tile
                            ]
                    for t in range(per_tile):
                        head = j * size + q * per_tile + t
                        column = (head % heads_piece) * HD
                        flat[f, head // heads_piece, place, column : column + HD] = parted[
                            q, t
                        ].astype(jnp.bfloat16)

    for f in range(HALVES):
        if f < HALVES - 1:
            pass_side(f)
        if f == max(HALVES - 2, 0):
            forward_all(HALVES - 1)
        if f == HALVES - 1:
            pass_side(f)
        bring(f)

        @pl.loop(0, out_blocks)
        def _(n):
            total = None
            for p in range(pieces):
                if f == 0:
                    out_copy(n, p).wait()
                product = jnp.dot(
                    flat[f, p], weights[n * pieces + p], preferred_element_type=jnp.float32
                )
                total = product if total is None else total + product
            own[f, n] = total.reshape(inner, part, cw)
            for d in range(inner - 1):
                to_sum[f, n, d] = own[f, n, lax.rem(gy + d + 1, inner)].astype(jnp.bfloat16)
                send_sum(f, n, d).start()

    for f in range(HALVES):

        @pl.loop(0, out_blocks)
        def _(n):
            for d in range(inner - 1):
                send_sum(f, n, d).wait()
            for c in range(cw // HD):
                columns = slice(c * HD, (c + 1) * HD)
                total = own[f, n, gy, :, columns]
                for d in range(inner - 1):
                    total = total + from_sum[f, n, d, :, columns].astype(jnp.float32)
                for q in range(part // tile):
                    for s in range(STEPS):
                        start = q * tile + s * half_rows
                        target = q * rows + f * half_rows
                        place = pl.ds(pl.multiple_of(n * cw + c * HD, HD), HD)
                        piece[s, target : target + half_rows, place] = total[
                            start : start + half_rows
                        ]

    for s in range(STEPS):
        result[s] = piece[s].astype(jnp.bfloat16)

    for f in range(HALVES):
        for d in range(inner):
            if d > 0:
                send_rows(f, d - 1).wait_send()
            for e in range(pairs - 1):
                gather(f, d, e).wait_send()
            for e in range(pairs):
                share(f, d, e).wait_send()


def body(x_first, x_second, norm_gain, w_qkv, w_out, cache_keys, cache_values, lengths):
    outer, inner = lax.axis_size("gx"), lax.axis_size("gy")
    rows, slots, kv_width = cache_keys.shape
    depth, in_columns = w_qkv.shape
    out_depth, out_columns = w_out.shape
    width = depth * outer
    heads = in_columns // HD
    groups = kv_width // HD // inner
    size = heads // groups - 2
    chunk_heads = 4 if in_columns % (4 * HD) == 0 and out_columns % (4 * HD) == 0 else 2
    chunks = heads // chunk_heads
    cw = chunk_heads * HD
    pairs = outer // 2
    here = STEPS * inner * rows
    tile = STEPS * rows // HALVES
    queries = size * tile // SUB
    total = outer * here // HALVES
    part = total // inner
    out_blocks = out_columns // cw
    pieces = out_depth // depth
    dims = (outer, inner, rows, width, groups, size, chunk_heads, chunks)

    half = HD // 2
    freq = rotary_base ** (-(np.arange(half, dtype=np.float64) * 2.0 / HD))
    freq = jnp.asarray(np.tile(freq, 2)[None], jnp.float32)

    dma = pltpu.SemaphoreType.DMA
    vmem = pl.BlockSpec(memory_space=pltpu.VMEM)
    away = pl.BlockSpec(memory_space=pl.ANY)
    f32, b16 = jnp.float32, jnp.bfloat16
    result = pl.pallas_call(
        functools.partial(block_kernel, dims),
        in_specs=[
            pl.BlockSpec(memory_space=pltpu.SMEM), away, away, vmem, vmem, away, away, away, away,
        ],
        out_specs=vmem,
        out_shape=jax.ShapeDtypeStruct((STEPS, HALVES * part // STEPS, out_columns), b16),
        scratch_shapes=[
            pltpu.VMEM((STEPS, outer * inner * rows, depth), b16),
            pltpu.VMEM((rows, slots + EXTRA, kv_width), b16),
            pltpu.VMEM((rows, slots + EXTRA, kv_width), b16),
            pltpu.VMEM((max(in_columns // cw, out_blocks * pieces), depth, cw), b16),
            pltpu.VMEM((outer * here, depth), b16),
            pltpu.VMEM((chunks, pairs, 2, here, cw), f32),
            pltpu.VMEM((chunks, pairs, here, cw), f32),
            pltpu.VMEM((chunks, HALVES, pairs - 1, here // HALVES, cw), b16),
            pltpu.VMEM((chunks, HALVES, pairs - 1, here // HALVES, cw), b16),
            pltpu.VMEM((pairs, 2, here, HD), f32),
            pltpu.VMEM((pairs, here, HD), f32),
            pltpu.VMEM((pairs - 1, here, HD), f32),
            pltpu.VMEM((pairs - 1, here, HD), f32),
            pltpu.VMEM((inner, chunk_heads * tile, HD), f32),
            pltpu.VMEM((chunks, HALVES, inner, chunk_heads * tile // SUB, SUB, HD), b16),
            pltpu.VMEM((inner, chunks, HALVES, chunk_heads * tile // SUB, SUB, HD), b16),
            pltpu.VMEM((groups, (size + 2) * tile, HD), f32),
            pltpu.VMEM((rows // HALVES, kv_width // HD * STEPS * size, kv_width), b16),
            pltpu.VMEM((rows // HALVES, 2, EXTRA, kv_width), f32),
            pltpu.VMEM((kv_width // HD, size * tile, HD), f32),
            pltpu.VMEM((HALVES, inner, groups, queries, SUB, HD), b16),
            pltpu.VMEM((HALVES, outer, inner, groups, queries, SUB, HD), b16),
            pltpu.VMEM((queries, SUB // tile, inner * tile, HD), f32),
            pltpu.VMEM((HALVES, pieces, total, depth), b16),
            pltpu.VMEM((HALVES, out_blocks, inner, part, cw), f32),
            pltpu.VMEM((HALVES, out_blocks, inner - 1, part, cw), b16),
            pltpu.VMEM((HALVES, out_blocks, inner - 1, part, cw), b16),
            pltpu.VMEM((STEPS, HALVES * part // STEPS, out_columns), f32),
            dma((STEPS,)), dma((2,)), dma((in_columns // cw,)), dma((out_blocks, pieces)),
            dma((chunks,)), dma((chunks,)),
            dma((chunks, HALVES, pairs - 1)), dma((chunks, HALVES, pairs - 1)),
            dma((chunks, HALVES, inner - 1)), dma((chunks, HALVES, inner - 1)),
            dma, dma, dma((pairs - 1,)), dma((pairs - 1,)), dma((chunks, HALVES)),
            dma((HALVES, inner - 1)), dma((HALVES, inner - 1)), dma((HALVES,)),
            dma((HALVES, inner, pairs - 1)), dma((HALVES, inner, pairs - 1)),
            dma((HALVES, inner, pairs)), dma((HALVES, inner, pairs)),
            dma((HALVES, out_blocks, inner - 1)), dma((HALVES, out_blocks, inner - 1)),
        ],
        compiler_params=pltpu.CompilerParams(
            collective_id=0, has_side_effects=True, vmem_limit_bytes=VMEM_LIMIT
        ),
        name="decode_block",
    )(lengths, x_first, x_second, norm_gain, freq, w_qkv, w_out, cache_keys, cache_values)
    return result[0], result[1]


def solution(mesh):
    in_specs = (
        P(None, "gx"),
        P(None, "gx"),
        P("gx"),
        P("gx", "gy"),
        P("gy", "gx"),
        P(("gx", "gy"), None, None),
        P(("gx", "gy"), None, None),
        P(("gx", "gy")),
    )
    out_specs = (P("gy", "gx"), P("gy", "gx"))
    return jax.shard_map(body, mesh=mesh, in_specs=in_specs, out_specs=out_specs, check_vma=False)
```

time: 82.7 us -> 72.9 us (0.88)
  Pallas kernels: 80 us -> 70.4 us
    pallas_call x1, Pallas kernels: 80 us -> 70.4 us  [body(): pl.pallas_call(functools.partial(block_kernel, dims), in_specs=[pl.BlockS...]
where the time goes in v3:
time: 72.9 us; the launch traced here: 72.7 us
  Pallas kernels  70.4 us (97%)
  local copies, waits for them, and re-layouts  1.68 us (2%)
    pallas_call x1, Pallas kernels, body(): pl.pallas_call(functools.partial(block_kernel, dims), in_specs=[pl.BlockS...  70.4 us
    squeeze x1, local copies, waits for them, and re-layouts, body(): return (result[0], result[1])  1.68 us

profile of v3, /device:TPU:0, one launch (start us, length us, event | category | flops | bytes accessed | tf_op | source)
XLA Modules:
  0.0 72.7 jit_solution(3964273190895178308)
XLA Ops:
  0.6 70.4 %decode_block.1 = bf16[2,32,2048]{2,1,0:T(8,128)(2,1)} custom-call(s32[4]{0:T(128)} %lengths.1, bf16[128,2048]{1,0:T(8,128)(2,1)} %x_first.1, bf16[128,2048]{1,0:T(8,128)(2,1)} %x_second.1, bf16[2048]{0:T(1024)(128)(2,1)} %gain.1, f32[1,128]{1,0:T(1,128)} %constant.2.clone.freq, bf16[2048,4608]{1,0:T(8,128)(2,1)} %w_in.1, bf16[4096,2048]{1,0:T(8,128)(2,1)} %w_out.1, ...), custom_call_target="tpu_custom_call" | custom-call | tf_op jit(solution)/shard_map/decode_block/pallas_call | solution.py:520
  71.0 1.7 %slice_bitcast_fusion = (bf16[32,2048]{1,0:T(8,128)(2,1)}, bf16[32,2048]{1,0:T(8,128)(2,1)}) fusion(bf16[2,32,2048]{2,1,0:T(8,128)(2,1)} %decode_block.1), kind=kLoop, calls=%fused_computation | loop fusion | bytes 524288 | tf_op jit(solution)/shard_map/squeeze | solution.py:571

commit v4 on v3

--- a/solution.py
+++ b/solution.py
@@ -75,8 +75,12 @@
                 pl.ds(p * depth, depth), pl.ds(pl.multiple_of(n * cw, cw), cw)
             ],
             weights.at[n * pieces + p],
-            out_sem.at[n, p],
-        )
+            out_sem.at[n],
+        )
+
+    def out_ready(n):
+        ref = weights.at[pl.ds(n * pieces, pieces)]
+        return pltpu.make_async_copy(ref, ref, out_sem.at[n])
 
     kv_copies = [
         pltpu.make_async_copy(keys, k_here.at[:, pl.ds(0, slots)], kv_sem.at[0]),
@@ -87,28 +91,28 @@
         return remote(sq.at[:, 1 - side], sq_other, sq_send, sq_recv, other)
 
     def send_sq_along(d):
-        return remote(sq_to.at[d], sq_along.at[d], sqa_send.at[d], sqa_recv.at[d], along[d])
+        return remote(sq_to.at[d], sq_along.at[d], sqa_send, sqa_recv, along[d])
 
     def send_pair(n):
         return remote(
-            prod.at[n, :, 1 - side], from_other.at[n], pair_send.at[n], pair_recv.at[n], other
+            prod.at[n, :, 1 - side], from_other.at[n], pair_send, pair_recv.at[n], other
         )
 
     def send_along(n, f, d):
         return remote(
             to_along.at[n, f, d], from_along.at[n, f, d],
-            along_send.at[n, f, d], along_recv.at[n, f, d], along[d],
+            along_send.at[f], along_recv.at[n, f], along[d],
         )
 
     def send_across(n, f, d):
         return remote(
             to_across.at[n, f, lax.rem(gy + d + 1, inner)], joined.at[gy, n, f],
-            across_send.at[n, f, d], across_recv.at[n, f, d], across[d],
+            across_send.at[f], across_recv.at[f], across[d],
         )
 
     def keep_own(n, f):
         return pltpu.make_async_copy(
-            to_across.at[n, f, gy], joined.at[gy, n, f], own_sem.at[n, f]
+            to_across.at[n, f, gy], joined.at[gy, n, f], own_sem.at[f]
         )
 
     def source(d):
@@ -116,7 +120,7 @@
 
     def send_rows(f, d):
         return remote(
-            to_rows.at[f, d], held.at[f, gx, gy], rows_send.at[f, d], rows_recv.at[f, d], across[d]
+            to_rows.at[f, d], held.at[f, gx, gy], rows_send.at[f], rows_recv.at[f, d], across[d]
         )
 
     def keep_rows(f):
@@ -126,17 +130,20 @@
 
     def gather(f, d, e):
         ref = held.at[f, gx, source(d)]
-        return remote(ref, ref, gather_send.at[f, d, e], gather_recv.at[f, d, e], along[e])
-
-    def share(f, d, e):
-        ref = held.at[f, 2 * lax.rem(pair + pairs - e, pairs) + side, source(d)]
-        return remote(ref, ref, share_send.at[f, d, e], share_recv.at[f, d, e], other)
+        return remote(ref, ref, gather_send.at[f], gather_recv.at[f, e], along[e])
+
+    def share(f, e):
+        ref = held.at[f, 2 * lax.rem(pair + pairs - e, pairs) + side]
+        return remote(ref, ref, share_send.at[f], share_recv.at[f, e], other)
 
     def send_sum(f, n, d):
         return remote(
             to_sum.at[f, n, d], from_sum.at[f, n, d],
-            sum_send.at[f, n, d], sum_recv.at[f, n, d], across[d],
-        )
+            sum_send.at[f], sum_recv.at[f, n], across[d],
+        )
+
+    def arrived(ref, sem):
+        pltpu.make_async_copy(ref, ref, sem).wait()
 
     for copy in x_copies:
         copy.start()
@@ -183,7 +190,7 @@
     send_sq().start()
 
     def pass_on(n):
-        send_pair(n).wait()
+        send_pair(n).wait_recv()
         for d in range(pairs - 1):
             there = lax.rem(pair + d + 1, pairs)
             both = (prod[n, there, side] + from_other[n, there]).astype(jnp.bfloat16)
@@ -224,8 +231,8 @@
             out_copy(n, p).start()
 
     squares = sq[pair, side] + sq_other[pair]
+    arrived(sq_along, sqa_recv)
     for d in range(pairs - 1):
-        send_sq_along(d).wait()
         squares = squares + sq_along[d]
     factor = lax.rsqrt(squares / width + norm_eps)
     for f in range(HALVES):
@@ -252,8 +259,7 @@
         sines.append(jnp.where(lane < HD // 2, -jnp.sin(angle), jnp.sin(angle)))
 
     def settle(n, f):
-        for d in range(pairs - 1):
-            send_along(n, f, d).wait()
+        arrived(from_along.at[n, f], along_recv.at[n, f])
         span = slice(f * half, (f + 1) * half)
         for h in range(chunk_heads):
             columns = slice(h * HD, (h + 1) * HD)
@@ -292,7 +298,6 @@
     def forward(f, d):
         for e in range(pairs - 1):
             gather(f, d, e).start()
-        share(f, d, 0).start()
 
     def forward_all(f):
         keep_rows(f).wait()
@@ -300,6 +305,7 @@
         for d in range(1, inner):
             send_rows(f, d - 1).wait_recv()
             forward(f, d)
+        share(f, 0).start()
 
     fresh[...] = jnp.zeros_like(fresh)
 
@@ -320,11 +326,8 @@
                 def _():
                     settle(n, f)
 
-        @pl.loop(0, chunks)
-        def _(n):
-            keep_own(n, f).wait()
-            for d in range(inner - 1):
-                send_across(n, f, d).wait()
+        arrived(joined.at[0, :, f], own_sem.at[f])
+        arrived(joined.at[pl.ds(0, inner - 1), :, f], across_recv.at[f])
 
         if f > 0:
             forward_all(f - 1)
@@ -402,15 +405,13 @@
     span = inner * tile
 
     def pass_side(f):
-        for d in range(inner):
-            for e in range(pairs - 1):
-                gather(f, d, e).wait_recv()
-                share(f, d, e + 1).start()
+        for e in range(pairs - 1):
+            arrived(held.at[f, 0], gather_recv.at[f, e])
+            share(f, e + 1).start()
 
     def bring(f):
-        for d in range(inner):
-            for e in range(pairs):
-                share(f, d, e).wait_recv()
+        for e in range(pairs):
+            share(f, e).wait_recv()
 
         @pl.loop(0, outer)
         def _(g):
@@ -442,9 +443,9 @@
         @pl.loop(0, out_blocks)
         def _(n):
             total = None
+            if f == 0:
+                out_ready(n).wait()
             for p in range(pieces):
-                if f == 0:
-                    out_copy(n, p).wait()
                 product = jnp.dot(
                     flat[f, p], weights[n * pieces + p], preferred_element_type=jnp.float32
                 )
@@ -458,8 +459,7 @@
 
         @pl.loop(0, out_blocks)
         def _(n):
-            for d in range(inner - 1):
-                send_sum(f, n, d).wait()
+            arrived(from_sum.at[f, n], sum_recv.at[f, n])
             for c in range(cw // HD):
                 columns = slice(c * HD, (c + 1) * HD)
                 total = own[f, n, gy, :, columns]
@@ -477,14 +477,15 @@
     for s in range(STEPS):
         result[s] = piece[s].astype(jnp.bfloat16)
 
+    arrived(prod.at[:, :, 0], pair_send)
+    arrived(sq_to, sqa_send)
     for f in range(HALVES):
-        for d in range(inner):
-            if d > 0:
-                send_rows(f, d - 1).wait_send()
-            for e in range(pairs - 1):
-                gather(f, d, e).wait_send()
-            for e in range(pairs):
-                share(f, d, e).wait_send()
+        arrived(to_along.at[:, f], along_send.at[f])
+        arrived(to_across.at[:, f, pl.ds(0, inner - 1)], across_send.at[f])
+        arrived(to_rows.at[f, pl.ds(0, inner - 1)], rows_send.at[f])
+        arrived(held.at[f, pl.ds(0, pairs - 1)], gather_send.at[f])
+        arrived(held.at[f, pl.ds(0, pairs)], share_send.at[f])
+        arrived(to_sum.at[f], sum_send.at[f])
 
 
 def body(x_first, x_second, norm_gain, w_qkv, w_out, cache_keys, cache_values, lengths):
@@ -553,15 +554,15 @@
             pltpu.VMEM((HALVES, out_blocks, inner - 1, part, cw), b16),
             pltpu.VMEM((HALVES, out_blocks, inner - 1, part, cw), b16),
             pltpu.VMEM((STEPS, HALVES * part // STEPS, out_columns), f32),
-            dma((STEPS,)), dma((2,)), dma((in_columns // cw,)), dma((out_blocks, pieces)),
-            dma((chunks,)), dma((chunks,)),
-            dma((chunks, HALVES, pairs - 1)), dma((chunks, HALVES, pairs - 1)),
-            dma((chunks, HALVES, inner - 1)), dma((chunks, HALVES, inner - 1)),
-            dma, dma, dma((pairs - 1,)), dma((pairs - 1,)), dma((chunks, HALVES)),
-            dma((HALVES, inner - 1)), dma((HALVES, inner - 1)), dma((HALVES,)),
-            dma((HALVES, inner, pairs - 1)), dma((HALVES, inner, pairs - 1)),
-            dma((HALVES, inner, pairs)), dma((HALVES, inner, pairs)),
-            dma((HALVES, out_blocks, inner - 1)), dma((HALVES, out_blocks, inner - 1)),
+            dma((STEPS,)), dma((2,)), dma((chunks,)), dma((out_blocks,)),
+            dma, dma((chunks,)),
+            dma((HALVES,)), dma((chunks, HALVES)),
+            dma((HALVES,)), dma((HALVES,)),
+            dma, dma, dma, dma, dma((HALVES,)),
+            dma((HALVES,)), dma((HALVES, inner - 1)), dma((HALVES,)),
+            dma((HALVES,)), dma((HALVES, pairs - 1)),
+            dma((HALVES,)), dma((HALVES, pairs)),
+            dma((HALVES,)), dma((HALVES, out_blocks)),
         ],
         compiler_params=pltpu.CompilerParams(
             collective_id=0, has_side_effects=True, vmem_limit_bytes=VMEM_LIMIT

time: 72.9 us -> 70.4 us (0.966)
  Pallas kernels: 70.4 us -> 67.9 us
    pallas_call x1, Pallas kernels: 70.4 us -> 67.9 us  [body(): pl.pallas_call(functools.partial(block_kernel, dims), in_specs=[pl.BlockS...]
where the time goes in v4:
time: 70.4 us; the launch traced here: 70.3 us
  Pallas kernels  67.9 us (96%)
  local copies, waits for them, and re-layouts  1.68 us (2%)
    pallas_call x1, Pallas kernels, body(): pl.pallas_call(functools.partial(block_kernel, dims), in_specs=[pl.BlockS...  67.9 us
    squeeze x1, local copies, waits for them, and re-layouts, body(): return (result[0], result[1])  1.68 us

profile of v4, /device:TPU:0, one launch (start us, length us, event | category | flops | bytes accessed | tf_op | source)
XLA Modules:
  0.0 70.3 jit_solution(14697339541730256023)
XLA Ops:
  0.6 67.9 %decode_block.1 = bf16[2,32,2048]{2,1,0:T(8,128)(2,1)} custom-call(s32[4]{0:T(128)} %lengths.1, bf16[128,2048]{1,0:T(8,128)(2,1)} %x_first.1, bf16[128,2048]{1,0:T(8,128)(2,1)} %x_second.1, bf16[2048]{0:T(1024)(128)(2,1)} %gain.1, f32[1,128]{1,0:T(1,128)} %constant.2.clone.freq, bf16[2048,4608]{1,0:T(8,128)(2,1)} %w_in.1, bf16[4096,2048]{1,0:T(8,128)(2,1)} %w_out.1, ...), custom_call_target="tpu_custom_call" | custom-call | tf_op jit(solution)/shard_map/decode_block/pallas_call | solution.py:521
  68.6 1.7 %slice_bitcast_fusion = (bf16[32,2048]{1,0:T(8,128)(2,1)}, bf16[32,2048]{1,0:T(8,128)(2,1)}) fusion(bf16[2,32,2048]{2,1,0:T(8,128)(2,1)} %decode_block.1), kind=kLoop, calls=%fused_computation | loop fusion | bytes 524288 | tf_op jit(solution)/shard_map/squeeze | solution.py:572

commit v5 on v4

--- a/solution.py
+++ b/solution.py
@@ -16,6 +16,7 @@
 HALVES = 2
 SUB = 8
 EXTRA = 16
+LAG = 2
 VMEM_LIMIT = 62 * 1024 * 1024
 MESH = pl.DeviceIdType.MESH
 
@@ -213,11 +214,13 @@
                 sq_to[d] = sq[there, side] + sq_other[there]
                 send_sq_along(d).start()
 
-        @pl.when(n > 0)
+        @pl.when(n >= LAG)
         def _():
-            pass_on(n - 1)
-
-    pass_on(chunks - 1)
+            pass_on(n - LAG)
+
+    @pl.loop(chunks - LAG, chunks)
+    def _(n):
+        pass_on(n)
 
     @pl.loop(0, chunks)
     def _(n):
@@ -300,8 +303,6 @@
             gather(f, d, e).start()
 
     def forward_all(f):
-        keep_rows(f).wait()
-        forward(f, 0)
         for d in range(1, inner):
             send_rows(f, d - 1).wait_recv()
             forward(f, d)
@@ -326,11 +327,10 @@
                 def _():
                     settle(n, f)
 
+        if f > 0:
+            forward_all(f - 1)
         arrived(joined.at[0, :, f], own_sem.at[f])
         arrived(joined.at[pl.ds(0, inner - 1), :, f], across_recv.at[f])
-
-        if f > 0:
-            forward_all(f - 1)
 
         @pl.loop(0, inner)
         def _(y):
@@ -400,6 +400,8 @@
             if d < inner - 1:
                 send_rows(f, d).start()
         keep_rows(f).start()
+        keep_rows(f).wait()
+        forward(f, 0)
 
     heads_piece = depth // HD
     span = inner * tile
@@ -473,9 +475,9 @@
                         piece[s, target : target + half_rows, place] = total[
                             start : start + half_rows
                         ]
-
-    for s in range(STEPS):
-        result[s] = piece[s].astype(jnp.bfloat16)
+                if f == HALVES - 1:
+                    for s in range(STEPS):
+                        result[s, :, place] = piece[s, :, place].astype(jnp.bfloat16)
 
     arrived(prod.at[:, :, 0], pair_send)
     arrived(sq_to, sqa_send)

time: 70.4 us -> 66.4 us (0.943)
  Pallas kernels: 67.9 us -> 63.9 us
    pallas_call x1, Pallas kernels: 67.9 us -> 63.9 us  [body(): pl.pallas_call(functools.partial(block_kernel, dims), in_specs=[pl.BlockS...]
where the time goes in v5:
time: 66.4 us; the launch traced here: 66.2 us
  Pallas kernels  63.9 us (96%)
  local copies, waits for them, and re-layouts  1.68 us (3%)
    pallas_call x1, Pallas kernels, body(): pl.pallas_call(functools.partial(block_kernel, dims), in_specs=[pl.BlockS...  63.9 us
    squeeze x1, local copies, waits for them, and re-layouts, body(): return (result[0], result[1])  1.68 us

profile of v5, /device:TPU:0, one launch (start us, length us, event | category | flops | bytes accessed | tf_op | source)
XLA Modules:
  0.0 66.2 jit_solution(885396579250979599)
XLA Ops:
  0.6 63.9 %decode_block.1 = bf16[2,32,2048]{2,1,0:T(8,128)(2,1)} custom-call(s32[4]{0:T(128)} %lengths.1, bf16[128,2048]{1,0:T(8,128)(2,1)} %x_first.1, bf16[128,2048]{1,0:T(8,128)(2,1)} %x_second.1, bf16[2048]{0:T(1024)(128)(2,1)} %gain.1, f32[1,128]{1,0:T(1,128)} %constant.2.clone.freq, bf16[2048,4608]{1,0:T(8,128)(2,1)} %w_in.1, bf16[4096,2048]{1,0:T(8,128)(2,1)} %w_out.1, ...), custom_call_target="tpu_custom_call" | custom-call | tf_op jit(solution)/shard_map/decode_block/pallas_call | solution.py:523
  64.5 1.7 %slice_bitcast_fusion = (bf16[32,2048]{1,0:T(8,128)(2,1)}, bf16[32,2048]{1,0:T(8,128)(2,1)}) fusion(bf16[2,32,2048]{2,1,0:T(8,128)(2,1)} %decode_block.1), kind=kLoop, calls=%fused_computation | loop fusion | bytes 524288 | tf_op jit(solution)/shard_map/squeeze | solution.py:574

commit v6 on v5

--- a/solution.py
+++ b/solution.py
@@ -17,6 +17,7 @@
 SUB = 8
 EXTRA = 16
 LAG = 2
+RELAYS = (2, 2)
 VMEM_LIMIT = 62 * 1024 * 1024
 MESH = pl.DeviceIdType.MESH
 
@@ -28,15 +29,20 @@
     )
 
 
+def relays_of(inner, out_blocks):
+    return RELAYS if inner == 4 and out_blocks > max(RELAYS) else (0,) * HALVES
+
+
 def block_kernel(
     dims, lengths, x_first, x_second, gain, freq, w_in, w_out, keys, values, result,
     x_here, k_here, v_here, weights, scaled, prod, from_other, to_along, from_along,
     sq, sq_other, sq_to, sq_along, mixed, to_across, joined,
     turned, spread, fresh, mix, to_rows, held, parted, flat, own, to_sum, from_sum, piece,
+    to_near, from_near, wide_near, wide_from, to_far, from_far,
     x_sem, kv_sem, in_sem, out_sem, pair_send, pair_recv, along_send, along_recv,
     across_send, across_recv, sq_send, sq_recv, sqa_send, sqa_recv, own_sem,
     rows_send, rows_recv, keep_sem, gather_send, gather_recv, share_send, share_recv,
-    sum_send, sum_recv,
+    sum_send, sum_recv, near_send, near_recv, wide_send, wide_recv, far_send, far_recv,
 ):
     outer, inner, rows, width, groups, size, chunk_heads, chunks = dims
     gx, gy = lax.axis_index("gx"), lax.axis_index("gy")
@@ -142,6 +148,22 @@
             to_sum.at[f, n, d], from_sum.at[f, n, d],
             sum_send.at[f], sum_recv.at[f, n], across[d],
         )
+
+    relays = relays_of(inner, out_blocks)
+    near = gy + 1 - 2 * lax.rem(gy, 2)
+    near_far, far = lax.rem(near + 2, inner), lax.rem(gy + 2, inner)
+
+    def relay_index(f, n):
+        return sum(relays[:f]) + n
+
+    def send_near(k):
+        return remote(to_near.at[k], from_near.at[k], near_send, near_recv.at[k], (gx, near))
+
+    def send_wide(k):
+        return remote(wide_near.at[k], wide_from.at[k], wide_send, wide_recv.at[k], (gx, near))
+
+    def send_far(k):
+        return remote(to_far.at[k], from_far.at[k], far_send, far_recv.at[k], (gx, far))
 
     def arrived(ref, sem):
         pltpu.make_async_copy(ref, ref, sem).wait()
@@ -442,8 +464,7 @@
             pass_side(f)
         bring(f)
 
-        @pl.loop(0, out_blocks)
-        def _(n):
+        def multiply(n):
             total = None
             if f == 0:
                 out_ready(n).wait()
@@ -453,31 +474,67 @@
                 )
                 total = product if total is None else total + product
             own[f, n] = total.reshape(inner, part, cw)
+
+        if relays[f]:
+
+            @pl.loop(0, relays[f])
+            def _(n):
+                multiply(n)
+                k = relay_index(f, n)
+                wide_near[k] = own[f, n, near_far]
+                send_wide(k).start()
+                to_near[k] = own[f, n, near].astype(jnp.bfloat16)
+                send_near(k).start()
+
+        @pl.loop(relays[f], out_blocks)
+        def _(n):
+            multiply(n)
             for d in range(inner - 1):
                 to_sum[f, n, d] = own[f, n, lax.rem(gy + d + 1, inner)].astype(jnp.bfloat16)
                 send_sum(f, n, d).start()
 
+        if relays[f]:
+
+            @pl.loop(0, relays[f])
+            def _(n):
+                k = relay_index(f, n)
+                send_wide(k).wait_recv()
+                to_far[k] = (own[f, n, far] + wide_from[k]).astype(jnp.bfloat16)
+                send_far(k).start()
+
     for f in range(HALVES):
 
-        @pl.loop(0, out_blocks)
-        def _(n):
-            arrived(from_sum.at[f, n], sum_recv.at[f, n])
+        def settle_sum(n, terms):
             for c in range(cw // HD):
                 columns = slice(c * HD, (c + 1) * HD)
                 total = own[f, n, gy, :, columns]
-                for d in range(inner - 1):
-                    total = total + from_sum[f, n, d, :, columns].astype(jnp.float32)
+                for term in terms:
+                    total = total + term[:, columns].astype(jnp.float32)
+                place = pl.ds(pl.multiple_of(n * cw + c * HD, HD), HD)
                 for q in range(part // tile):
                     for s in range(STEPS):
                         start = q * tile + s * half_rows
                         target = q * rows + f * half_rows
-                        place = pl.ds(pl.multiple_of(n * cw + c * HD, HD), HD)
                         piece[s, target : target + half_rows, place] = total[
                             start : start + half_rows
                         ]
                 if f == HALVES - 1:
                     for s in range(STEPS):
                         result[s, :, place] = piece[s, :, place].astype(jnp.bfloat16)
+
+        if relays[f]:
+
+            @pl.loop(0, relays[f])
+            def _(n):
+                k = relay_index(f, n)
+                send_near(k).wait_recv()
+                send_far(k).wait_recv()
+                settle_sum(n, [from_near.at[k], from_far.at[k]])
+
+        @pl.loop(relays[f], out_blocks)
+        def _(n):
+            arrived(from_sum.at[f, n], sum_recv.at[f, n])
+            settle_sum(n, [from_sum.at[f, n, d] for d in range(inner - 1)])
 
     arrived(prod.at[:, :, 0], pair_send)
     arrived(sq_to, sqa_send)
@@ -487,7 +544,11 @@
         arrived(to_rows.at[f, pl.ds(0, inner - 1)], rows_send.at[f])
         arrived(held.at[f, pl.ds(0, pairs - 1)], gather_send.at[f])
         arrived(held.at[f, pl.ds(0, pairs)], share_send.at[f])
-        arrived(to_sum.at[f], sum_send.at[f])
+        arrived(to_sum.at[f, pl.ds(relays[f], out_blocks - relays[f])], sum_send.at[f])
+    if sum(relays):
+        arrived(to_near, near_send)
+        arrived(wide_near, wide_send)
+        arrived(to_far, far_send)
 
 
 def body(x_first, x_second, norm_gain, w_qkv, w_out, cache_keys, cache_values, lengths):
@@ -510,6 +571,7 @@
     part = total // inner
     out_blocks = out_columns // cw
     pieces = out_depth // depth
+    relayed = max(1, sum(relays_of(inner, out_blocks)))
     dims = (outer, inner, rows, width, groups, size, chunk_heads, chunks)
 
     half = HD // 2
@@ -556,6 +618,12 @@
             pltpu.VMEM((HALVES, out_blocks, inner - 1, part, cw), b16),
             pltpu.VMEM((HALVES, out_blocks, inner - 1, part, cw), b16),
             pltpu.VMEM((STEPS, HALVES * part // STEPS, out_columns), f32),
+            pltpu.VMEM((relayed, part, cw), b16),
+            pltpu.VMEM((relayed, part, cw), b16),
+            pltpu.VMEM((relayed, part, cw), f32),
+            pltpu.VMEM((relayed, part, cw), f32),
+            pltpu.VMEM((relayed, part, cw), b16),
+            pltpu.VMEM((relayed, part, cw), b16),
             dma((STEPS,)), dma((2,)), dma((chunks,)), dma((out_blocks,)),
             dma, dma((chunks,)),
             dma((HALVES,)), dma((chunks, HALVES)),
@@ -565,6 +633,7 @@
             dma((HALVES,)), dma((HALVES, pairs - 1)),
             dma((HALVES,)), dma((HALVES, pairs)),
             dma((HALVES,)), dma((HALVES, out_blocks)),
+            dma, dma((relayed,)), dma, dma((relayed,)), dma, dma((relayed,)),
         ],
         compiler_params=pltpu.CompilerParams(
             collective_id=0, has_side_effects=True, vmem_limit_bytes=VMEM_LIMIT

time: 66.4 us -> 63.8 us (0.961); the launches traced: 66.2 us -> 62.5 us
  Pallas kernels: 63.9 us -> 60.2 us
    pallas_call x1, Pallas kernels: 63.9 us -> 60.2 us  [body(): pl.pallas_call(functools.partial(block_kernel, dims), in_specs=[pl.BlockS...]
where the time goes in v6:
time: 63.8 us; the launch traced here: 62.5 us
  Pallas kernels  60.2 us (94%)
  local copies, waits for them, and re-layouts  1.68 us (3%)
  between operations  0.64 us (1%)
    pallas_call x1, Pallas kernels, body(): pl.pallas_call(functools.partial(block_kernel, dims), in_specs=[pl.BlockS...  60.2 us
    squeeze x1, local copies, waits for them, and re-layouts, body(): return (result[0], result[1])  1.68 us

profile of v6, /device:TPU:0, one launch (start us, length us, event | category | flops | bytes accessed | tf_op | source)
XLA Modules:
  0.0 62.5 jit_solution(6876053403492428184)
XLA Ops:
  0.6 60.2 %decode_block.1 = bf16[2,32,2048]{2,1,0:T(8,128)(2,1)} custom-call(s32[4]{0:T(128)} %lengths.1, bf16[128,2048]{1,0:T(8,128)(2,1)} %x_first.1, bf16[128,2048]{1,0:T(8,128)(2,1)} %x_second.1, bf16[2048]{0:T(1024)(128)(2,1)} %gain.1, f32[1,128]{1,0:T(1,128)} %constant.2.clone.freq, bf16[2048,4608]{1,0:T(8,128)(2,1)} %w_in.1, bf16[4096,2048]{1,0:T(8,128)(2,1)} %w_out.1, ...), custom_call_target="tpu_custom_call" | custom-call | tf_op jit(solution)/shard_map/decode_block/pallas_call | solution.py:585
  60.8 1.7 %slice_bitcast_fusion = (bf16[32,2048]{1,0:T(8,128)(2,1)}, bf16[32,2048]{1,0:T(8,128)(2,1)}) fusion(bf16[2,32,2048]{2,1,0:T(8,128)(2,1)} %decode_block.1), kind=kLoop, calls=%fused_computation | loop fusion | bytes 524288 | tf_op jit(solution)/shard_map/squeeze | solution.py:643

commit v7 on v6

--- a/solution.py
+++ b/solution.py
@@ -434,11 +434,15 @@
             share(f, e + 1).start()
 
     def bring(f):
+        fill(f, side)
         for e in range(pairs):
             share(f, e).wait_recv()
-
-        @pl.loop(0, outer)
-        def _(g):
+        fill(f, 1 - side)
+
+    def fill(f, which):
+        @pl.loop(0, pairs)
+        def _(c):
+            g = 2 * c + which
             place = pl.ds(pl.multiple_of(g * span, span), span)
             for j in range(groups):
                 for q in range(queries):
@@ -455,6 +459,16 @@
                             q, t
                         ].astype(jnp.bfloat16)
 
+    def relay_on(f):
+        if relays[f]:
+
+            @pl.loop(0, relays[f])
+            def _(n):
+                k = relay_index(f, n)
+                send_wide(k).wait_recv()
+                to_far[k] = (own[f, n, far] + wide_from[k]).astype(jnp.bfloat16)
+                send_far(k).start()
+
     for f in range(HALVES):
         if f < HALVES - 1:
             pass_side(f)
@@ -462,6 +476,7 @@
             forward_all(HALVES - 1)
         if f == HALVES - 1:
             pass_side(f)
+            relay_on(f - 1)
         bring(f)
 
         def multiply(n):
@@ -493,14 +508,8 @@
                 to_sum[f, n, d] = own[f, n, lax.rem(gy + d + 1, inner)].astype(jnp.bfloat16)
                 send_sum(f, n, d).start()
 
-        if relays[f]:
-
-            @pl.loop(0, relays[f])
-            def _(n):
-                k = relay_index(f, n)
-                send_wide(k).wait_recv()
-                to_far[k] = (own[f, n, far] + wide_from[k]).astype(jnp.bfloat16)
-                send_far(k).start()
+        if f == HALVES - 1:
+            relay_on(f)
 
     for f in range(HALVES):
 
@@ -588,7 +597,7 @@
             pl.BlockSpec(memory_space=pltpu.SMEM), away, away, vmem, vmem, away, away, away, away,
         ],
         out_specs=vmem,
-        out_shape=jax.ShapeDtypeStruct((STEPS, HALVES * part // STEPS, out_columns), b16),
+        out_shape=pltpu.VMEM((STEPS, HALVES * part // STEPS, out_columns), b16),
         scratch_shapes=[
             pltpu.VMEM((STEPS, outer * inner * rows, depth), b16),
             pltpu.VMEM((rows, slots + EXTRA, kv_width), b16),

time: 63.8 us -> 62.9 us (0.986); the launches traced: 62.5 us -> 62.7 us
  Pallas kernels: 60.2 us -> 61.3 us
  local copies, waits for them, and re-layouts: 1.68 us -> 0.72 us
    pallas_call x1, Pallas kernels: 60.2 us -> 61.3 us  [body(): pl.pallas_call(functools.partial(block_kernel, dims), in_specs=[pl.BlockS...]
    squeeze x1, local copies, waits for them, and re-layouts: 1.68 us -> 0.72 us  [body(): return (result[0], result[1])]
where the time goes in v7:
time: 62.9 us; the launch traced here: 62.7 us
  Pallas kernels  61.3 us (97%)
  local copies, waits for them, and re-layouts  0.72 us (1%)
  between operations  0.64 us (1%)
    pallas_call x1, Pallas kernels, body(): pl.pallas_call(functools.partial(block_kernel, dims), in_specs=[pl.BlockS...  61.3 us

profile of v7, /device:TPU:0, one launch (start us, length us, event | category | flops | bytes accessed | tf_op | source)
XLA Modules:
  0.0 62.7 jit_solution(4509250964925355087)
XLA Ops:
  0.6 61.3 %decode_block.1 = bf16[2,32,2048]{2,1,0:T(8,128)(2,1)S(1)} custom-call(s32[4]{0:T(128)} %lengths.1, bf16[128,2048]{1,0:T(8,128)(2,1)} %x_first.1, bf16[128,2048]{1,0:T(8,128)(2,1)} %x_second.1, bf16[2048]{0:T(1024)(128)(2,1)} %gain.1, f32[1,128]{1,0:T(1,128)} %constant.2.clone.freq, bf16[2048,4608]{1,0:T(8,128)(2,1)} %w_in.1, bf16[4096,2048]{1,0:T(8,128)(2,1)} %w_out.1, ...), custom_call_target="tpu_custom_call" | custom-call | tf_op jit(solution)/shard_map/decode_block/pallas_call | solution.py:594
  62.0 0.7 %slice_bitcast_fusion = (bf16[32,2048]{1,0:T(8,128)(2,1)}, bf16[32,2048]{1,0:T(8,128)(2,1)}) fusion(bf16[2,32,2048]{2,1,0:T(8,128)(2,1)S(1)} %decode_block.1), kind=kLoop, calls=%fused_computation | loop fusion | bytes 524288 | tf_op jit(solution)/shard_map/squeeze | solution.py:652

commit v8 on v7

--- a/solution.py
+++ b/solution.py
@@ -137,7 +137,8 @@
 
     def gather(f, d, e):
         ref = held.at[f, gx, source(d)]
-        return remote(ref, ref, gather_send.at[f], gather_recv.at[f, e], along[e])
+        origin = to_rows.at[f, inner - 1] if d == 0 else ref
+        return remote(origin, ref, gather_send.at[f], gather_recv.at[f, e], along[e])
 
     def share(f, e):
         ref = held.at[f, 2 * lax.rem(pair + pairs - e, pairs) + side]
@@ -328,6 +329,7 @@
         for d in range(1, inner):
             send_rows(f, d - 1).wait_recv()
             forward(f, d)
+        keep_rows(f).wait()
         share(f, 0).start()
 
     fresh[...] = jnp.zeros_like(fresh)
@@ -422,7 +424,6 @@
             if d < inner - 1:
                 send_rows(f, d).start()
         keep_rows(f).start()
-        keep_rows(f).wait()
         forward(f, 0)
 
     heads_piece = depth // HD

time: 62.9 us -> 62.9 us (level)
  no operation moved by 1% of the time
where the time goes in v8:
time: 62.9 us; the launch traced here: 62.7 us
  Pallas kernels  61.3 us (97%)
  local copies, waits for them, and re-layouts  0.72 us (1%)
  between operations  0.64 us (1%)
    pallas_call x1, Pallas kernels, body(): pl.pallas_call(functools.partial(block_kernel, dims), in_specs=[pl.BlockS...  61.3 us

profile of v8, /device:TPU:0, one launch (start us, length us, event | category | flops | bytes accessed | tf_op | source)
XLA Modules:
  0.0 62.7 jit_solution(1474186662654389065)
XLA Ops:
  0.6 61.3 %decode_block.1 = bf16[2,32,2048]{2,1,0:T(8,128)(2,1)S(1)} custom-call(s32[4]{0:T(128)} %lengths.1, bf16[128,2048]{1,0:T(8,128)(2,1)} %x_first.1, bf16[128,2048]{1,0:T(8,128)(2,1)} %x_second.1, bf16[2048]{0:T(1024)(128)(2,1)} %gain.1, f32[1,128]{1,0:T(1,128)} %constant.2.clone.freq, bf16[2048,4608]{1,0:T(8,128)(2,1)} %w_in.1, bf16[4096,2048]{1,0:T(8,128)(2,1)} %w_out.1, ...), custom_call_target="tpu_custom_call" | custom-call | tf_op jit(solution)/shard_map/decode_block/pallas_call | solution.py:595
  62.0 0.7 %slice_bitcast_fusion = (bf16[32,2048]{1,0:T(8,128)(2,1)}, bf16[32,2048]{1,0:T(8,128)(2,1)}) fusion(bf16[2,32,2048]{2,1,0:T(8,128)(2,1)S(1)} %decode_block.1), kind=kLoop, calls=%fused_computation | loop fusion | bytes 524288 | tf_op jit(solution)/shard_map/squeeze | solution.py:653
